TPU v7x, 512 devices: a whole 4x4x16 slice. The times are simulated.
512 devices in a mesh: tm: 16 (over z), expert: 32 (over x, y, core).
Axes of the slice: x: 4, y: 4, z: 16, core: 2. Of those that a mesh axis runs over, the one named last changes fastest.
Arguments:
- x_in: float32 [32, 4096, 1024], P('expert', 'tm'), may hold values from -6 to 6
- z_gate: bfloat16 [32, 4096, 1024], P('expert', 'tm'), may hold values from -6 to 6
- b_proj: float32 [32, 4096, 128], P('expert', 'tm'), may hold values from -1.5 to 1.5
- c_proj: float32 [32, 4096, 128], P('expert', 'tm'), may hold values from -1.5 to 1.5
- decay_log: float32 [32, 4096, 16], P('expert', 'tm'), as said below
- skip_gain: float32 [16], replicated, may hold values from 0.5 to 2
- residual: float32 [32, 4096, 1024], P('expert', 'tm'), may hold values from -6 to 6
- ssd_gain: float32 [1024], replicated, may hold values from 0.5 to 1.5
- moe_gain: float32 [1024], replicated, may hold values from 0.5 to 1.5
- w_gate: bfloat16 [32, 1024, 1536], P('expert', 'tm'), may hold values from -0.1875 to 0.1875
- w_up: bfloat16 [32, 1024, 1536], P('expert', 'tm'), may hold values from -0.1875 to 0.1875
- w_down: bfloat16 [32, 1536, 1024], P('expert', 'tm'), may hold values from -0.15625 to 0.15625
- routes: int32 [32, 4096, 2], P('expert', 'tm'), may hold values from 0 to 31, all different within a row; in each aligned block of 256 rows (0 to 255, 256 to 511, ..., all dimensions but the last counted through in order) at most 24 rows name the same one
- route_weights: float32 [32, 4096, 2], P('expert', 'tm'), may hold values from 0.2 to 1
Outputs:
- mixed: float32 [32, 4096, 1024], P('expert', 'tm')
Inputs may be any that keep to these rules, and one draw needn't show every extreme that they name: `routes`: the two experts of a time step differ. Among the time steps of one device no expert is named more than 24 times, and in every draw some device names some expert exactly 24 times. `decay_log`: every entry is at most zero.
All inputs are finite; a program needn't handle non-finite values.
Results may differ from a plain program's by a relative error of at most 0.0021.
Values may be sent and summed in bfloat16 or wider, within the bound.
No kernel may reach another device: no remote copies, remote signals or barrier semaphores. Data moves between devices by JAX's collectives and lax.ppermute only.
A program may use at most 64 MiB of HBM per device.

v0:
```python
import math

import jax
import jax.numpy as jnp
from jax import lax
from jax.sharding import PartitionSpec as P

exact_mode = lax.Precision.HIGHEST


def carried_in_2(value, axis, join, neutral):
    count, mine = (lax.axis_size(axis), lax.axis_index(axis))
    pieces = jax.tree.map(lambda part: lax.all_gather(part, axis), value)
    running = jax.tree.map(
        lambda part, zero: jnp.full_like(part, 0) + jnp.asarray(zero, part.dtype), value, neutral
    )

    def lap(position, running):
        longer = join(running, jax.tree.map(lambda part: part[position], pieces))
        return jax.tree.map(lambda new, old: jnp.where(position < mine, new, old), longer, running)

    return lax.fori_loop(0, count - 1, lap, running)


def group_carry(state, values, b_rows, running):
    remains = jnp.exp(running[-1][None, :] - running)
    fresh = jnp.einsum("jhp,jn->hpn", values * remains[:, :, None], b_rows, precision=exact_mode)
    return jnp.exp(running[-1])[:, None, None] * state + fresh


def group_step(state, inputs, skip_gain):
    values, b_rows, c_rows, log_rates = inputs
    length = values.shape[0]
    running = jnp.cumsum(log_rates, axis=0)
    across = running.T[:, :, None] - running.T[:, None, :]
    places = jnp.arange(length)
    causal = (places[:, None] >= places[None, :])[None]
    masked = jnp.where(causal, jnp.exp(jnp.where(causal, across, 0.0)), 0.0)
    scores = jnp.dot(c_rows, b_rows.T, precision=exact_mode)
    mixing = masked * scores[None]
    output = jnp.einsum("hij,jhp->ihp", mixing, values, precision=exact_mode)
    output = output + jnp.exp(running)[:, :, None] * jnp.einsum(
        "in,hpn->ihp", c_rows, state, precision=exact_mode
    )
    output = output + skip_gain[None, :, None] * values
    return (group_carry(state, values, b_rows, running), output)


def incoming_state(through, local_end):

    def combine(earlier, later):
        return (earlier[0] * later[0], later[0][:, None, None] * earlier[1] + later[1])

    prefix = carried_in_2(
        (through, local_end), "tm", combine, (jnp.ones_like(through), jnp.zeros_like(local_end))
    )
    return prefix[1]


def rms_scale(rows, gain):
    return gain * rows / jnp.sqrt(jnp.mean(rows * rows, axis=-1, keepdims=True) + 1e-05)


def per_device(
    x_in,
    z_gate,
    b_proj,
    c_proj,
    decay_log,
    skip_gain,
    residual,
    ssd_gain,
    moe_gain,
    w_gate,
    w_up,
    w_down,
    routes,
    route_weights,
):
    heads = skip_gain.shape[0]
    model_width = x_in.shape[2]
    width = model_width // heads
    length = x_in.shape[1]
    block = math.gcd(length, 256)
    count = length // block
    values = x_in[0].reshape(length, heads, width)
    b_rows = b_proj[0]
    c_rows = c_proj[0]
    log_rates = decay_log[0]
    inputs = (
        values.reshape(count, block, heads, width),
        b_rows.reshape(count, block, -1),
        c_rows.reshape(count, block, -1),
        log_rates.reshape(count, block, heads),
    )
    start = jnp.zeros((heads, width, b_rows.shape[1]), jnp.float32)
    through = jnp.exp(jnp.sum(log_rates, axis=0))
    local_end, outputs = lax.scan(
        lambda state, piece: group_step(state, piece, skip_gain), start, inputs
    )
    incoming = incoming_state(through, local_end)
    running = jnp.cumsum(log_rates, axis=0)
    carried_in = jnp.exp(running)[:, :, None] * jnp.einsum(
        "in,hpn->ihp", c_rows, incoming, precision=exact_mode
    )
    mixed_ssd = (outputs.reshape(length, heads, width) + carried_in).reshape(length, model_width)
    gated = mixed_ssd * jax.nn.silu(z_gate[0].astype(jnp.float32))
    hres = residual[0] + rms_scale(gated, ssd_gain)
    normed = rms_scale(hres, moe_gain).astype(jnp.bfloat16)
    expert_count = lax.axis_size("expert")
    capacity = max(2, 3 * length // expert_count)
    flat_routes = routes[0].reshape(-1)
    picked_one = (flat_routes[:, None] == jnp.arange(expert_count)[None, :]).astype(jnp.int32)
    earlier_hits = jnp.cumsum(picked_one, axis=0) - picked_one
    slot_index = jnp.sum(earlier_hits * picked_one, axis=1)
    target = flat_routes * capacity + slot_index
    repeated = jnp.broadcast_to(normed[:, None, :], (length, 2, model_width)).reshape(
        2 * length, model_width
    )
    outgoing = (
        jnp.zeros((expert_count * capacity, model_width), jnp.bfloat16).at[target].set(repeated)
    )
    received = lax.all_to_all(
        outgoing.reshape(expert_count, capacity, model_width),
        "expert",
        split_axis=0,
        concat_axis=0,
        tiled=True,
    )
    received = received.reshape(expert_count * capacity, model_width)
    slot_rows = expert_count * capacity
    columns = received
    gate = jnp.dot(
        columns,
        lax.all_gather(w_gate[0], "tm", axis=0, tiled=True),
        preferred_element_type=jnp.float32,
    )
    upper = jnp.dot(
        columns,
        lax.all_gather(w_up[0], "tm", axis=0, tiled=True),
        preferred_element_type=jnp.float32,
    )
    hidden = (jax.nn.silu(gate) * upper).astype(jnp.bfloat16)
    columns = hidden
    produced = jnp.dot(
        columns,
        lax.all_gather(w_down[0], "tm", axis=0, tiled=True),
        preferred_element_type=jnp.float32,
    ).astype(jnp.bfloat16)
    back = lax.all_to_all(
        produced.reshape(expert_count, capacity, model_width),
        "expert",
        split_axis=0,
        concat_axis=0,
        tiled=True,
    )
    back = back.reshape(slot_rows, model_width)
    fetched = back[target].astype(jnp.float32).reshape(length, 2, model_width)
    weights_here = route_weights[0]
    moe = fetched[:, 0, :] * weights_here[:, 0:1] + fetched[:, 1, :] * weights_here[:, 1:2]
    return (hres + moe).reshape(1, length, model_width)


def solution(mesh):
    in_specs = (
        P("expert", "tm", None),
        P("expert", "tm", None),
        P("expert", "tm", None),
        P("expert", "tm", None),
        P("expert", "tm", None),
        P(),
        P("expert", "tm", None),
        P(),
        P(),
        P("expert", "tm", None),
        P("expert", "tm", None),
        P("expert", "tm", None),
        P("expert", "tm", None),
        P("expert", "tm", None),
    )
    out_specs = P("expert", "tm", None)
    return jax.shard_map(
        per_device, mesh=mesh, in_specs=in_specs, out_specs=out_specs, check_vma=False
    )
```

profile of v0, /device:TPU:1, one launch (start us, length us, event | category | flops | bytes accessed | tf_op | source)
XLA Modules:
  0.0 405.9 jit_solution(9429766804105325587)
XLA Ops:
  6.5 0.8 copy_bitcast_fusion.3
  7.3 0.6 reduce-window.16
  8.5 1.6 copy.54
  10.2 1.8 convolution_add_fusion
  12.0 0.7 all-gather.12.cloned.1.call-update
  12.8 0.7 all-gather.14.cloned.1.call-update
  15.0 1.3 dynamic-slice
  17.1 32.2 %all-reduce = f32[256]{0:T(256)S(1)} all-reduce(f32[256]{0:T(256)S(1)} %exponential_dynamic-update-slice_fusion), channel_id=2, replica_groups=mesh['tm'=16,'expert'=32] {'tm'}, use_global_device_ids=true, to_apply=%add | all-reduce | flops 256 | bytes 2048
  49.4 1.2 copy.57
  50.6 1.2 reduce-window.24
  52.4 5.1 %fusion.24 = f32[256,16,64]{0,2,1:T(8,128)S(1)} fusion(f32[256,16,64]{0,2,1:T(8,128)S(1)} %bitcast.161, f32[256,256]{1,0:T(8,128)S(1)} %fusion.49, f32[16,256]{1,0:T(8,128)S(1)} %get-tuple-element.159, pred[256,256]{1,0:T(8,128)(4,1)S(1)} %iota_compare_fusion), kind=kOutput, calls=%fused_computation.23 | convolution fusion | flops 809500672 | bytes 2441216 | tf_op jit(solution)/shard_map/while/body/eval_jaxpr/hij,jhp->ihp/dot_general | solution.py:41
  57.6 2.1 fusion.31
  59.7 64.1 %all-gather.10.cloned.1.call-done = f32[256,64,128]{2,1,0:T(8,128)} async-done(((f32[16,64,128]{2,1,0:T(8,128)}), f32[256,64,128]{2,1,0:T(8,128)}) %all-gather.10.cloned.1.call-update) | async-done | bytes 8388624 | tf_op jit(solution)/shard_map/all_gather | solution.py:13
  123.7 18.2 %while.9 = (s32[]{:T(128)}, f32[16,64,128]{2,1,0:T(8,128)S(1)}, s32[]{:T(128)}, f32[16,16]{1,0:T(8,128)S(1)}, f32[16,16,64,128]{3,2,1,0:T(8,128)}, /*index=5*/s32[]{:T(128)}, s32[]{:T(128)}) while((s32[]{:T(128)}, f32[16,64,128]{2,1,0:T(8,128)S(1)}, s32[]{:T(128)}, f32[16,16]{1,0:T(8,128)S(1)}, f32[16,16,64,128]{3,2,1,0:T(8,128)}, ...), condition=%wide.region_4.5_spmd.clone, body=%wide.region_3.4_spmd.clone.sunk | while | flops 524292 | bytes 1573161 | solution.py:22
  123.8 1.2 fusion.70
  125.0 1.2 fusion.70
  126.2 1.2 fusion.70
  127.4 1.2 fusion.70
  128.6 1.2 fusion.70
  129.8 1.2 fusion.70
  131.0 1.2 fusion.70
  132.2 1.2 fusion.70
  133.5 1.2 fusion.70
  134.7 1.2 fusion.70
  135.9 1.2 fusion.70
  137.1 1.2 fusion.70
  138.3 1.2 fusion.70
  139.5 1.2 fusion.70
  140.8 1.2 fusion.70
  142.0 2.8 multiply_reduce_fusion.1
  144.8 1.3 copy.62
  146.1 1.8 multiply_reduce_fusion
  148.1 0.5 broadcast_in_dim.66
  148.7 1.2 reshape.351
  149.9 4.5 %scatter_custom_fusion = bf16[768,1024]{1,0:T(8,128)(2,1)} fusion(s32[512]{0:T(512)S(1)} %bitcast.171, bf16[512,1024]{1,0:T(8,128)(2,1)} %reshape.351, bf16[]{:T(256)} %constant.72.clone.1), kind=kCustom, calls=%fused_computation.51 | custom fusion | bytes 1573376 | tf_op jit(solution)/shard_map/scatter | solution.py:121
  154.4 7.5 %all-to-all-start = ((bf16[32,24,1024]{2,1,0:T(8,128)(2,1)}), bf16[32,24,1024]{2,1,0:T(8,128)(2,1)S(1)}, u32[]{:S(2)}, u32[]{:S(2)}) async-start(bf16[32,24,1024]{2,1,0:T(8,128)(2,1)} %bitcast.23), calls=%async_computation | async-start | bytes 3145728 | tf_op jit(solution)/shard_map/all_to_all | solution.py:123
  162.0 29.4 %all-gather.12.cloned.1.call-done = bf16[1,1024,1536]{2,1,0:T(8,128)(2,1)} async-done(((bf16[1,64,1536]{2,1,0:T(8,128)(2,1)}), bf16[1,1024,1536]{2,1,0:T(8,128)(2,1)}) %all-gather.12.cloned.1.call-update) | async-done | bytes 3145744 | tf_op jit(solution)/shard_map/all_gather | solution.py:135
  191.3 6.1 %fusion.10 = f32[768,1536]{1,0:T(8,128)} fusion(bf16[768,1024]{1,0:T(8,128)(2,1)S(1)} %bitcast.166, bf16[1,1024,1536]{2,1,0:T(8,128)(2,1)} %all-gather.12.cloned.1.call-done), kind=kOutput, calls=%fused_computation.15 | convolution fusion | flops 2415919104 | bytes 9437184 | tf_op jit(solution)/shard_map/dot_general | solution.py:133
  197.4 69.0 %all-gather.14.cloned.1.call-done = bf16[1,1024,1536]{2,1,0:T(8,128)(2,1)} async-done(((bf16[1,64,1536]{2,1,0:T(8,128)(2,1)}), bf16[1,1024,1536]{2,1,0:T(8,128)(2,1)}) %all-gather.14.cloned.1.call-update) | async-done | bytes 3145744 | tf_op jit(solution)/shard_map/all_gather | solution.py:140
  266.4 75.2 %all-gather.16.cloned.1.call-done = bf16[1,1536,1024]{2,1,0:T(8,128)(2,1)} async-done(((bf16[1,96,1024]{2,1,0:T(8,128)(2,1)}), bf16[1,1536,1024]{2,1,0:T(8,128)(2,1)}) %all-gather.16.cloned.1.call-update) | async-done | bytes 3145744 | tf_op jit(solution)/shard_map/all_gather | solution.py:147
  341.6 10.5 %fusion.19 = bf16[768,1024]{1,0:T(8,128)(2,1)} fusion(bf16[1,1536,1024]{2,1,0:T(8,128)(2,1)} %all-gather.16.cloned.1.call-done, f32[768,1536]{1,0:T(8,128)} %fusion.10, bf16[768,1024]{1,0:T(8,128)(2,1)S(1)} %bitcast.167, bf16[1,1024,1536]{2,1,0:T(8,128)(2,1)} %all-gather.14.cloned.1.call-done), kind=kOutput, calls=%fused_computation.22 | convolution fusion | flops 4839702528 | bytes 14155776 | tf_op jit(solution)/shard_map/dot_general | solution.py:145
  352.0 16.2 %all-to-all-start.1 = ((bf16[32,24,1024]{2,1,0:T(8,128)(2,1)}), bf16[32,24,1024]{2,1,0:T(8,128)(2,1)S(1)}, u32[]{:S(2)}, u32[]{:S(2)}) async-start(bf16[32,24,1024]{2,1,0:T(8,128)(2,1)} %bitcast.168), calls=%async_computation.1 | async-start | bytes 3145728 | tf_op jit(solution)/shard_map/all_to_all | solution.py:150
  368.3 1.3 copy.56
  369.6 21.3 %all-to-all-done.1 = bf16[32,24,1024]{2,1,0:T(8,128)(2,1)S(1)} async-done(((bf16[32,24,1024]{2,1,0:T(8,128)(2,1)}), bf16[32,24,1024]{2,1,0:T(8,128)(2,1)S(1)}, u32[]{:S(2)}, u32[]{:S(2)}) %all-to-all-start.1) | async-done | bytes 1572896 | tf_op jit(solution)/shard_map/all_to_all | solution.py:150
  390.9 2.8 gather_fusion
  393.7 2.4 reshape.338
  396.1 1.6 fusion.61
  397.7 1.6 fusion.34
  (78 shorter events, 3.5 us)
Async XLA Ops:
  6.5 8.1 %copy-start = (f32[1,256,128]{2,1,0:T(8,128)S(1)}, f32[1,256,128]{2,1,0:T(8,128)}, u32[]{:S(2)}) copy-start(f32[1,256,128]{2,1,0:T(8,128)} %param.19) | copy-start | bytes 393220
  6.5 3.6 copy-start.5
  6.5 117.2 %all-gather.10.cloned.1.call-start = ((), (), s32[]{:S(2)}) async-start(), calls=%async_computation.2 | async-start | bytes 8912896 | tf_op jit(solution)/shard_map/all_gather | solution.py:13
  8.4 5.6 %copy-start.6 = (f32[1,256,16]{1,2,0:T(8,128)S(1)}, f32[1,256,16]{1,2,0:T(8,128)}, u32[]{:S(2)}) copy-start(f32[1,256,16]{1,2,0:T(8,128)} %param.20) | copy-start | bytes 49156
  8.5 5.7 %copy-start.8 = (s32[1,256,2]{1,2,0:T(2,128)S(1)}, s32[1,256,2]{1,2,0:T(2,128)}, u32[]{:S(2)}) copy-start(s32[1,256,2]{1,2,0:T(2,128)} %param.28) | copy-start | bytes 6148
  10.0 39.4 %copy-start.1 = (bf16[1,256,1024]{2,1,0:T(8,128)(2,1)S(1)}, bf16[1,256,1024]{2,1,0:T(8,128)(2,1)}, u32[]{:S(2)}) copy-start(bf16[1,256,1024]{2,1,0:T(8,128)(2,1)} %param.17) | copy-start | bytes 1572868
  12.0 179.4 %all-gather.12.cloned.1.call-start = ((), (), s32[]{:S(2)}) async-start(), calls=%async_computation.3 | async-start | bytes 3342336 | tf_op jit(solution)/shard_map/all_gather | solution.py:135
  12.7 253.7 %all-gather.14.cloned.1.call-start = ((), (), s32[]{:S(2)}) async-start(), calls=%async_computation.4 | async-start | bytes 3342336 | tf_op jit(solution)/shard_map/all_gather | solution.py:140
  13.4 328.1 %all-gather.16.cloned.1.call-start = ((), (), s32[]{:S(2)}) async-start(), calls=%async_computation.5 | async-start | bytes 3342336 | tf_op jit(solution)/shard_map/all_gather | solution.py:147
  52.4 5.1 %copy-start.11 = (f32[16]{0:T(128)S(1)}, f32[16]{0:T(128)}, u32[]{:S(2)}) copy-start(f32[16]{0:T(128)} %param.21) | copy-start | bytes 196
  142.0 4.2 %copy-start.3 = (f32[1,256,1024]{2,1,0:T(8,128)S(1)}, f32[1,256,1024]{2,1,0:T(8,128)}, u32[]{:S(2)}) copy-start(f32[1,256,1024]{2,1,0:T(8,128)} %param.22) | copy-start | bytes 3145732
  142.0 4.1 %copy-start.7 = (f32[1024]{0:T(1024)S(1)}, f32[1024]{0:T(1024)}, u32[]{:S(2)}) copy-start(f32[1024]{0:T(1024)} %param.23) | copy-start | bytes 12292
  144.8 3.1 copy-start.9
  154.4 36.9 %all-to-all-start = ((bf16[32,24,1024]{2,1,0:T(8,128)(2,1)}), bf16[32,24,1024]{2,1,0:T(8,128)(2,1)S(1)}, u32[]{:S(2)}, u32[]{:S(2)}) async-start(bf16[32,24,1024]{2,1,0:T(8,128)(2,1)} %bitcast.23), calls=%async_computation | async-start | bytes 3145728 | tf_op jit(solution)/shard_map/all_to_all | solution.py:123
  352.0 16.2 %copy-start.10 = (f32[1,256,2]{1,2,0:T(2,128)S(1)}, f32[1,256,2]{1,2,0:T(2,128)}, u32[]{:S(2)}) copy-start(f32[1,256,2]{1,2,0:T(2,128)} %param.29) | copy-start | bytes 6148
  352.0 38.9 %all-to-all-start.1 = ((bf16[32,24,1024]{2,1,0:T(8,128)(2,1)}), bf16[32,24,1024]{2,1,0:T(8,128)(2,1)S(1)}, u32[]{:S(2)}, u32[]{:S(2)}) async-start(bf16[32,24,1024]{2,1,0:T(8,128)(2,1)} %bitcast.168), calls=%async_computation.1 | async-start | bytes 3145728 | tf_op jit(solution)/shard_map/all_to_all | solution.py:150
  396.1 1.7 copy-start.2
  396.1 1.7 copy-start.4
Sparse Core Ops, SparseCore 0:
  12.1 111.6 all-gather.9
  125.8 65.4 all-gather.11
  193.4 72.9 all-gather.13
  268.3 73.2 all-gather.15
where the time goes:
time: 407 us; the launch traced here: 406 us
  waiting for transfers between devices  261 us (64%)
  blocking collectives  32.2 us (8%)
  matrix products  28.7 us (7%)
  starting transfers between devices  23.9 us (6%)
  other arithmetic  23.6 us (6%)
  local copies, waits for them, and re-layouts  22.1 us (5%)
  between operations  14.1 us (3%)
    all_gather x1, waiting for transfers between devices, per_device(): lax.all_gather(w_down[0], 'tm', axis=0, tiled=True)  75.2 us
    all_gather x1, waiting for transfers between devices, per_device(): lax.all_gather(w_up[0], 'tm', axis=0, tiled=True)  69 us
    all_gather x1, waiting for transfers between devices, carried_in_2(): pieces = jax.tree.map(lambda part: lax.all_gather(part, axis), value)  64.1 us
    unnamed x1, blocking collectives  32.2 us
    all_gather x1, waiting for transfers between devices, per_device(): lax.all_gather(w_gate[0], 'tm', axis=0, tiled=True)  29.4 us
    all_to_all x1, waiting for transfers between devices, per_device(): lax.all_to_all(produced.reshape(expert_count, capacity, model_width), 'ex...  21.3 us
    select_n x15, other arithmetic, lap(): jnp.where(position < mine, new, old)  17.6 us
    all_to_all x1, starting transfers between devices, per_device(): lax.all_to_all(produced.reshape(expert_count, capacity, model_width), 'ex...  16.2 us
  transfers between devices with their start and end apart: 6, of which 5 were waited for; matrix products, arithmetic and copies ran while one was open for 12% of the time, Pallas kernels for 0%

commit v1 on v0

v1 whole, which is shorter than its diff:
```python
import jax
import jax.numpy as jnp
from jax import lax
from jax.experimental import pallas as pl
from jax.experimental.pallas import tpu as pltpu
from jax.sharding import PartitionSpec as P

exact_mode = lax.Precision.HIGHEST
bf16 = jnp.bfloat16
f32 = jnp.float32
MIB = 1 << 20

f16 = jnp.float16
HEAD_PAD = 8
SPLIT = 2048.0
FF_BLOCK = 512
OUT_BLOCK = 512


def rms_scale(rows, gain):
    return gain * rows / jnp.sqrt(jnp.mean(rows * rows, axis=-1, keepdims=True) + 1e-05)


def pack_weights(gate, up, down):
    moves, row = [], 0
    for which, piece, step in ((0, gate, FF_BLOCK), (1, up, FF_BLOCK), (2, down, OUT_BLOCK)):
        for column in range(0, piece.shape[1], step):
            moves.append((which, column, row, piece.shape[0]))
            row += piece.shape[0]

    def body(gate_ref, up_ref, down_ref, out_ref, sems):
        sources = (gate_ref, up_ref, down_ref)
        copies = [
            pltpu.make_async_copy(
                sources[which].at[:, column : column + FF_BLOCK],
                out_ref.at[first : first + rows, :],
                sems.at[i],
            )
            for i, (which, column, first, rows) in enumerate(moves)
        ]
        for copy in copies:
            copy.start()
        for copy in copies:
            copy.wait()

    anywhere = pl.BlockSpec(memory_space=pl.ANY)
    return pl.pallas_call(
        body,
        in_specs=[anywhere] * 3,
        out_specs=anywhere,
        out_shape=jax.ShapeDtypeStruct((row, FF_BLOCK), gate.dtype),
        scratch_shapes=[pltpu.SemaphoreType.DMA((len(moves),))],
    )(gate, up, down)


def scan_states(received):
    count, padded, state = received.shape
    width = padded - HEAD_PAD

    def body(in_ref, out_ref):
        running = jnp.zeros((width, state), f32)
        for z in range(count):
            out_ref[z] = running.astype(out_ref.dtype)
            if z + 1 < count:
                tail = in_ref[z, width:padded, :].astype(f32)
                decay = tail[0:1, :] + (tail[1:2, :] + tail[2:3, :] / SPLIT) / SPLIT
                running = decay * running + in_ref[z, 0:width, :].astype(f32)

    return pl.pallas_call(
        body, out_shape=jax.ShapeDtypeStruct((count, width, state), received.dtype)
    )(received)


def expert_layer(rows, weights, model_width, hidden_width):
    total = rows.shape[0]
    parts = weights.shape[0]
    k_rows = model_width // parts
    f_rows = hidden_width // parts
    ff_steps = hidden_width // FF_BLOCK
    out_steps = model_width // OUT_BLOCK
    down_first = (2 * ff_steps * k_rows) // f_rows
    row_block = 256

    def body(x_ref, g_ref, u_ref, d_ref, out_ref, hid_ref):
        step = pl.program_id(0)
        for f in range(ff_steps):

            @pl.when(step == f)
            def _(f=f):
                wg = g_ref[...].reshape(model_width, FF_BLOCK)
                wu = u_ref[...].reshape(model_width, FF_BLOCK)
                for r in range(0, total, row_block):
                    x = x_ref[r : r + row_block, :]
                    gate = jnp.dot(x, wg, preferred_element_type=f32)
                    upper = jnp.dot(x, wu, preferred_element_type=f32)
                    hidden = (gate / (1.0 + jnp.exp(-gate))) * upper
                    hid_ref[r : r + row_block, f * FF_BLOCK : (f + 1) * FF_BLOCK] = hidden.astype(bf16)

        @pl.when(step >= ff_steps)
        def _():
            wd = d_ref[...].reshape(hidden_width, OUT_BLOCK)
            for r in range(0, total, row_block):
                out_ref[r : r + row_block, :] = jnp.dot(
                    hid_ref[r : r + row_block, :], wd, preferred_element_type=f32
                ).astype(bf16)

    last = ff_steps - 1
    return pl.pallas_call(
        body,
        grid=(ff_steps + out_steps,),
        in_specs=[
            pl.BlockSpec((total, model_width), lambda i: (0, 0)),
            pl.BlockSpec((parts, k_rows, FF_BLOCK), lambda i: (0, jnp.minimum(i, last), 0)),
            pl.BlockSpec((parts, k_rows, FF_BLOCK), lambda i: (0, ff_steps + jnp.minimum(i, last), 0)),
            pl.BlockSpec(
                (parts, f_rows, OUT_BLOCK),
                lambda i: (0, down_first + jnp.maximum(i - ff_steps, 0), 0),
            ),
        ],
        out_specs=pl.BlockSpec((total, OUT_BLOCK), lambda i: (0, jnp.maximum(i - ff_steps, 0))),
        out_shape=jax.ShapeDtypeStruct((total, model_width), bf16),
        scratch_shapes=[pltpu.VMEM((total, hidden_width), bf16)],
        compiler_params=pltpu.CompilerParams(vmem_limit_bytes=40 * MIB),
    )(rows, *[pltpu.with_memory_space_constraint(weights, pltpu.HBM)] * 3)


def combine(back, hres, targets, route_weights):
    slots, model_width = back.shape
    length = hres.shape[0]
    block = 256

    def body(back_ref, hres_ref, target_ref, weight_ref, out_ref, sel_ref):
        @pl.when(pl.program_id(0) == 0)
        def _():
            places = lax.broadcasted_iota(jnp.int32, (length, slots), 1)
            for k in range(2):
                sel_ref[k] = jnp.where(target_ref[:, k : k + 1] == places, 1.0, 0.0).astype(bf16)

        back_block = back_ref[...]
        first = jnp.dot(sel_ref[0], back_block, preferred_element_type=f32)
        second = jnp.dot(sel_ref[1], back_block, preferred_element_type=f32)
        out_ref[...] = hres_ref[...] + (weight_ref[:, 0:1] * first + weight_ref[:, 1:2] * second)

    return pl.pallas_call(
        body,
        grid=(model_width // block,),
        in_specs=[
            pl.BlockSpec((slots, block), lambda i: (0, i)),
            pl.BlockSpec((length, block), lambda i: (0, i)),
            pl.BlockSpec((length, 2), lambda i: (0, 0)),
            pl.BlockSpec((length, 2), lambda i: (0, 0)),
        ],
        out_specs=pl.BlockSpec((length, block), lambda i: (0, i)),
        out_shape=jax.ShapeDtypeStruct((length, model_width), f32),
        scratch_shapes=[pltpu.VMEM((2, length, slots), bf16)],
        compiler_params=pltpu.CompilerParams(vmem_limit_bytes=32 * MIB),
    )(back, hres, targets, route_weights)


def per_device(
    x_in,
    z_gate,
    b_proj,
    c_proj,
    decay_log,
    skip_gain,
    residual,
    ssd_gain,
    moe_gain,
    w_gate,
    w_up,
    w_down,
    routes,
    route_weights,
):
    heads = skip_gain.shape[0]
    length, model_width = x_in.shape[1], x_in.shape[2]
    width = model_width // heads
    hidden_width = w_gate.shape[2]
    experts = lax.axis_size("expert")
    capacity = max(2, 3 * length // experts)

    gathered = lax.all_gather(pack_weights(w_gate[0], w_up[0], w_down[0]), "tm", axis=0)

    values = x_in[0].reshape(length, heads, width)
    b_rows = b_proj[0]
    c_rows = c_proj[0]
    running = jnp.cumsum(decay_log[0], axis=0)

    remains = jnp.exp(running[-1][None, :] - running)
    local_end = jnp.einsum("jhp,jn->hpn", values * remains[:, :, None], b_rows, precision=exact_mode)
    through = jnp.exp(running[-1])
    part_a = lax.reduce_precision(through, 5, 10)
    rest = (through - part_a) * SPLIT
    part_b = lax.reduce_precision(rest, 5, 10)
    part_c = (rest - part_b) * SPLIT
    zero = jnp.zeros_like(through)
    tail = jnp.stack([part_a, part_b, part_c] + [zero] * (HEAD_PAD - 3), axis=1)
    tail = jnp.broadcast_to(tail[:, :, None], (heads, HEAD_PAD, b_rows.shape[1]))
    outgoing_state = jnp.concatenate([local_end, tail], axis=1).astype(f16)
    by_head = lax.all_to_all(outgoing_state, "tm", 0, 0, tiled=True).astype(f32)
    incoming = lax.all_to_all(scan_states(by_head).astype(f16), "tm", 0, 0, tiled=True).astype(f32)

    across = running.T[:, :, None] - running.T[:, None, :]
    places = jnp.arange(length)
    causal = (places[:, None] >= places[None, :])[None]
    masked = jnp.where(causal, jnp.exp(jnp.where(causal, across, 0.0)), 0.0)
    scores = jnp.dot(c_rows, b_rows.T, precision=exact_mode)
    inside = jnp.einsum("hij,jhp->ihp", masked * scores[None], values, precision=exact_mode)
    inside = inside + skip_gain[None, :, None] * values

    carried = jnp.exp(running)[:, :, None] * jnp.einsum(
        "in,hpn->ihp", c_rows, incoming, precision=exact_mode
    )
    mixed_ssd = (inside + carried).reshape(length, model_width)
    gated = mixed_ssd * jax.nn.silu(z_gate[0].astype(f32))
    hres = residual[0] + rms_scale(gated, ssd_gain)
    normed = rms_scale(hres, moe_gain).astype(bf16)

    chosen = routes[0]
    expert_ids = jnp.arange(experts)
    hit = (chosen[:, 0:1] == expert_ids) | (chosen[:, 1:2] == expert_ids)
    before = (places[:, None] > places[None, :]).astype(bf16)
    rank = jnp.dot(before, hit.astype(bf16), preferred_element_type=f32).astype(jnp.int32)
    slot = jnp.sum(
        jnp.where(chosen[:, :, None] == expert_ids[None, None, :], rank[:, None, :], 0), axis=2
    )
    targets = chosen * capacity + slot
    slot_ids = jnp.arange(experts * capacity)
    spread = (
        (targets[:, 0][None, :] == slot_ids[:, None]) | (targets[:, 1][None, :] == slot_ids[:, None])
    ).astype(bf16)
    outgoing = jnp.dot(spread, normed, preferred_element_type=f32).astype(bf16)
    received = lax.all_to_all(
        outgoing.reshape(experts, capacity, model_width), "expert", 0, 0, tiled=True
    )
    produced = expert_layer(
        received.reshape(experts * capacity, model_width), gathered, model_width, hidden_width
    )
    back = lax.all_to_all(
        produced.reshape(experts, capacity, model_width), "expert", 0, 0, tiled=True
    )
    out = combine(back.reshape(experts * capacity, model_width), hres, targets, route_weights[0])
    return out.reshape(1, length, model_width)


def solution(mesh):
    split = P("expert", "tm", None)
    in_specs = (split,) * 5 + (P(), split, P(), P()) + (split,) * 5
    return jax.shard_map(
        per_device, mesh=mesh, in_specs=in_specs, out_specs=split, check_vma=False
    )
```

time: 407 us -> 224 us (0.55)
  waiting for transfers between devices: 261 us -> 84.2 us
  Pallas kernels: 0 us -> 35.4 us
  local copies, waits for them, and re-layouts: 22.1 us -> 4.51 us
  matrix products: 28.7 us -> 11.7 us
  other arithmetic: 23.6 us -> 7.4 us
  starting transfers between devices: 23.9 us -> 32 us
    all_gather x4 -> x1, waiting for transfers between devices: 238 us -> 32.3 us  [per_device(): lax.all_gather(pack_weights(w_gate[0], w_up[0], w_down[0]), 'tm', axis=0)]
    pallas_call x0 -> x4, Pallas kernels: none -> 35.4 us  [the longest x1 19 us: pack_weights(): pl.pallas_call(body, in_specs=[anywhere] * 3, out_specs=anywhere, out_sha...]
    all_to_all x0 -> x1, blocking collectives: none -> 34.1 us  [per_device(): lax.all_to_all(outgoing.reshape(experts, capacity, model_width), 'expert'...]
    unnamed x1 -> x0, blocking collectives: 32.2 us -> none
    all_to_all x2 -> x3, waiting for transfers between devices: 21.3 us -> 51.9 us  [the longest x1 22.5 us: per_device(): lax.all_to_all(produced.reshape(experts, capacity, model_width), 'expert'...]
    select_n x16 -> x0, other arithmetic: 17.6 us -> none  [the longest x15 17.6 us: lap(): jnp.where(position < mine, new, old)]
    dot_general x6 -> x5, matrix products: 25.9 us -> 9.39 us  [the longest x1 7.06 us: per_device(): jnp.einsum('hij,jhp->ihp', masked * scores[None], values, precision=exact...]
    all_to_all x2 -> x3, starting transfers between devices: 23.8 us -> 32 us  [the longest x1 15.7 us: per_device(): by_head = lax.all_to_all(outgoing_state, 'tm', 0, 0, tiled=True).astype(f32)]
  transfers between devices with their start and end apart: 6 -> 4, of which waited for: 5 -> 4; matrix products, arithmetic and copies ran while one was open for 12% -> 11% of each run, Pallas kernels for 0% -> 1%
where the time goes in v1:
time: 224 us; the launch traced here: 223 us
  waiting for transfers between devices  84.2 us (38%)
  Pallas kernels  35.4 us (16%)
  blocking collectives  34.1 us (15%)
  starting transfers between devices  32 us (14%)
  between operations  13.6 us (6%)
  matrix products  11.7 us (5%)
  other arithmetic  7.4 us (3%)
  local copies, waits for them, and re-layouts  4.51 us (2%)
    all_to_all x1, blocking collectives, per_device(): lax.all_to_all(outgoing.reshape(experts, capacity, model_width), 'expert'...  34.1 us
    all_gather x1, waiting for transfers between devices, per_device(): lax.all_gather(pack_weights(w_gate[0], w_up[0], w_down[0]), 'tm', axis=0)  32.3 us
    all_to_all x1, waiting for transfers between devices, per_device(): lax.all_to_all(produced.reshape(experts, capacity, model_width), 'expert'...  22.5 us
    all_to_all x1, waiting for transfers between devices, per_device(): by_head = lax.all_to_all(outgoing_state, 'tm', 0, 0, tiled=True).astype(f32)  19.2 us
    pallas_call x1, Pallas kernels, pack_weights(): pl.pallas_call(body, in_specs=[anywhere] * 3, out_specs=anywhere, out_sha...  19 us
    all_to_all x1, starting transfers between devices, per_device(): by_head = lax.all_to_all(outgoing_state, 'tm', 0, 0, tiled=True).astype(f32)  15.7 us
    pallas_call x1, Pallas kernels, expert_layer(): pl.pallas_call(body, grid=(ff_steps + out_steps,), in_specs=[pl.BlockSpec...  11.5 us
    all_to_all x1, waiting for transfers between devices, per_device(): lax.all_to_all(scan_states(by_head).astype(f16), 'tm', 0, 0, tiled=True)  10.1 us
  transfers between devices with their start and end apart: 4, of which 4 were waited for; matrix products, arithmetic and copies ran while one was open for 11% of the time, Pallas kernels for 1%

profile of v1, /device:TPU:1, one launch (start us, length us, event | category | flops | bytes accessed | tf_op | source)
XLA Modules:
  0.0 222.9 jit_solution(12472007361213563873)
XLA Ops:
  6.5 0.0 copy-start
  6.5 0.0 all-gather.3.cloned.1.call-start
  6.5 19.0 %shard_map.137 = bf16[576,512]{1,0:T(8,128)(2,1)} custom-call(bf16[64,1536]{1,0:T(8,128)(2,1)} %bitcast.118, bf16[64,1536]{1,0:T(8,128)(2,1)} %bitcast.119, bf16[96,1024]{1,0:T(8,128)(2,1)} %bitcast.120), custom_call_target="tpu_custom_call" | custom-call | tf_op jit(solution)/shard_map/pallas_call | solution.py:47
  25.6 0.0 all-gather.3.cloned.1.call-update
  25.6 0.7 copy_bitcast_fusion.1
  26.3 0.6 reduce-window.6
  26.9 0.2 slice_reduce_fusion.4
  27.1 0.1 fusion.44
  27.2 0.2 slice_reduce_fusion.5
  27.4 0.1 copy.60
  27.5 0.1 copy.61
  27.6 0.1 copy.62
  27.7 0.1 stack.10
  27.8 1.6 copy.58
  29.3 0.7 bitcast_exponential_fusion
  30.0 0.1 bitcast_multiply_fusion.1
  30.1 1.0 convolution_convert_fusion.1
  31.1 0.1 broadcast_in_dim.32
  31.2 0.8 pad_maximum_fusion
  32.0 15.7 %all-to-all-start = ((f16[16,72,128]{2,1,0:T(8,128)(2,1)}), f16[16,72,128]{2,1,0:T(8,128)(2,1)S(1)}, u32[]{:S(2)}, u32[]{:S(2)}) async-start(f16[16,72,128]{2,1,0:T(8,128)(2,1)} %pad_maximum_fusion), calls=%async_computation | async-start | bytes 589824 | tf_op jit(solution)/shard_map/all_to_all | solution.py:201
  47.7 0.1 copy.53
  47.9 0.1 copy.54
  48.0 0.2 slice_reduce_fusion.3
  48.2 0.3 convolution_convert_fusion.2
  48.5 19.2 %all-to-all-done = f16[16,72,128]{2,1,0:T(8,128)(2,1)S(1)} async-done(((f16[16,72,128]{2,1,0:T(8,128)(2,1)}), f16[16,72,128]{2,1,0:T(8,128)(2,1)S(1)}, u32[]{:S(2)}, u32[]{:S(2)}) %all-to-all-start) | async-done | bytes 294944 | tf_op jit(solution)/shard_map/all_to_all | solution.py:201
  67.7 0.9 convert_element_type.33.in_ref
  68.6 1.9 shard_map.136
  70.5 1.8 convert_element_type.34
  72.3 8.7 %all-to-all-start.1 = ((f16[16,64,128]{2,1,0:T(8,128)(2,1)}), f16[16,64,128]{2,1,0:T(8,128)(2,1)S(1)}, u32[]{:S(2)}, u32[]{:S(2)}) async-start(f16[16,64,128]{2,1,0:T(8,128)(2,1)} %convert_element_type.34), calls=%async_computation.1 | async-start | bytes 524288 | tf_op jit(solution)/shard_map/all_to_all | solution.py:202
  81.0 0.6 iota_compare_fusion.3
  81.6 0.2 copy.64
  81.8 0.1 copy.55
  82.0 0.2 slice_reduce_fusion.1
  82.2 0.4 fusion.34
  82.6 7.1 %fusion.16 = f32[256,16,64]{0,2,1:T(8,128)} fusion(f32[256,16,64]{0,2,1:T(8,128)S(1)} %bitcast.111, f32[256,256]{1,0:T(8,128)S(1)} %fusion.34, f32[16,256]{1,0:T(8,128)S(1)} %get-tuple-element.16, pred[256,256]{1,0:T(8,128)(4,1)} %iota_compare_fusion.3, f32[16]{0:T(128)} %param.19), kind=kOutput, calls=%fused_computation.16 | convolution fusion | flops 810024960 | bytes 2441280 | tf_op jit(solution)/shard_map/hij,jhp->ihp/dot_general | solution.py:209
  89.7 10.1 %all-to-all-done.1 = f16[16,64,128]{2,1,0:T(8,128)(2,1)S(1)} async-done(((f16[16,64,128]{2,1,0:T(8,128)(2,1)}), f16[16,64,128]{2,1,0:T(8,128)(2,1)S(1)}, u32[]{:S(2)}, u32[]{:S(2)}) %all-to-all-start.1) | async-done | bytes 262176 | tf_op jit(solution)/shard_map/all_to_all | solution.py:202
  99.8 2.3 %multiply_reduce_fusion.1 = (f32[256]{0:T(256)S(1)}, f32[256,16,64]{0,2,1:T(8,128)S(1)}) fusion(f32[256,16,64]{0,2,1:T(8,128)S(1)} %bitcast.116, f32[256,16,64]{0,2,1:T(8,128)} %fusion.16, f16[16,64,128]{2,1,0:T(8,128)(2,1)S(1)} %all-to-all-done.1, f32[1,256,128]{2,1,0:T(8,128)S(1)} %copy-done, f32[256,16]{0,1:T(8,128)S(1)} %copy-done.3), kind=kOutput, calls=%fused_computation.31 | convolution fusion | flops 405012224 | bytes 3556352 | tf_op jit(solution)/shard_map/in,hpn->ihp/dot_general | solution.py:212
  102.1 0.0 copy-start.7
  102.1 0.3 copy.63
  102.4 1.8 multiply_reduce_fusion
  104.2 0.7 convolution_convert_fusion
  104.9 34.1 %all_to_all.20 = bf16[32,24,1024]{2,1,0:T(8,128)(2,1)S(1)} all-to-all(bf16[32,24,1024]{2,1,0:T(8,128)(2,1)S(1)} %bitcast.115), channel_id=1, replica_groups=mesh['tm'=16,'expert'=32] {'expert'}, dimensions={0} | all-to-all | bytes 3145728 | tf_op jit(solution)/shard_map/all_to_all | solution.py:234
  139.0 32.3 %all-gather.3.cloned.1.call-done = bf16[9216,512]{1,0:T(8,128)(2,1)} async-done(((bf16[576,512]{1,0:T(8,128)(2,1)}), bf16[9216,512]{1,0:T(8,128)(2,1)}) %all-gather.3.cloned.1.call-update) | async-done | bytes 9437200 | tf_op jit(solution)/shard_map/all_gather | solution.py:183
  171.3 11.5 %shard_map.138 = bf16[768,1024]{1,0:T(8,128)(2,1)} custom-call(bf16[768,1024]{1,0:T(8,128)(2,1)S(1)} %bitcast.106, bf16[16,576,512]{2,1,0:T(8,128)(2,1)} %bitcast.108, bf16[16,576,512]{2,1,0:T(8,128)(2,1)} %bitcast.109, bf16[16,576,512]{2,1,0:T(8,128)(2,1)} %bitcast.110), custom_call_target="tpu_custom_call" | custom-call | tf_op jit(solution)/shard_map/pallas_call | solution.py:108
  182.8 7.6 %all-to-all-start.3 = ((bf16[32,24,1024]{2,1,0:T(8,128)(2,1)}), bf16[32,24,1024]{2,1,0:T(8,128)(2,1)S(1)}, u32[]{:S(2)}, u32[]{:S(2)}) async-start(bf16[32,24,1024]{2,1,0:T(8,128)(2,1)} %bitcast.23), calls=%async_computation.3 | async-start | bytes 3145728 | tf_op jit(solution)/shard_map/all_to_all | solution.py:240
  190.4 0.1 copy.65
  190.5 22.5 %all-to-all-done.3 = bf16[32,24,1024]{2,1,0:T(8,128)(2,1)S(1)} async-done(((bf16[32,24,1024]{2,1,0:T(8,128)(2,1)}), bf16[32,24,1024]{2,1,0:T(8,128)(2,1)S(1)}, u32[]{:S(2)}, u32[]{:S(2)}) %all-to-all-start.3) | async-done | bytes 1572896 | tf_op jit(solution)/shard_map/all_to_all | solution.py:240
  213.1 3.0 %shard_map.139 = f32[256,1024]{1,0:T(8,128)} custom-call(bf16[768,1024]{1,0:T(8,128)(2,1)S(1)} %bitcast.105, f32[256,1024]{1,0:T(8,128)S(1)} %get-tuple-element.12.hres_ref, s32[256,2]{1,0:T(8,128)S(1)} %multiply_add_fusion.target_ref, f32[256,2]{1,0:T(8,128)S(1)} %bitcast.107), custom_call_target="tpu_custom_call" | custom-call | tf_op jit(solution)/shard_map/pallas_call | solution.py:144
  (24 shorter events, 0.2 us)
Async XLA Ops:
  6.5 75.7 %copy-start = (f32[1,256,128]{2,1,0:T(8,128)S(1)}, f32[1,256,128]{2,1,0:T(8,128)}, u32[]{:S(2)}) copy-start(f32[1,256,128]{2,1,0:T(8,128)} %param.17) | copy-start | bytes 393220
  6.5 23.6 %copy-start.2 = (f32[1,256,128]{2,1,0:T(8,128)S(1)}, f32[1,256,128]{2,1,0:T(8,128)}, u32[]{:S(2)}) copy-start(f32[1,256,128]{2,1,0:T(8,128)} %param.16) | copy-start | bytes 393220
  6.5 164.8 %all-gather.3.cloned.1.call-start = ((), (), s32[]{:S(2)}) async-start(), calls=%async_computation.4 | async-start | bytes 10027008 | tf_op jit(solution)/shard_map/all_gather | solution.py:183
  6.5 41.2 %copy-start.5 = (s32[1,256,2]{1,2,0:T(2,128)S(1)}, s32[1,256,2]{1,2,0:T(2,128)}, u32[]{:S(2)}) copy-start(s32[1,256,2]{1,2,0:T(2,128)} %param.26) | copy-start | bytes 6148
  30.0 51.6 %copy-start.1 = (bf16[1,256,1024]{2,1,0:T(8,128)(2,1)S(1)}, bf16[1,256,1024]{2,1,0:T(8,128)(2,1)}, u32[]{:S(2)}) copy-start(bf16[1,256,1024]{2,1,0:T(8,128)(2,1)} %param.15) | copy-start | bytes 1572868
  32.0 35.7 %all-to-all-start = ((f16[16,72,128]{2,1,0:T(8,128)(2,1)}), f16[16,72,128]{2,1,0:T(8,128)(2,1)S(1)}, u32[]{:S(2)}, u32[]{:S(2)}) async-start(f16[16,72,128]{2,1,0:T(8,128)(2,1)} %pad_maximum_fusion), calls=%async_computation | async-start | bytes 589824 | tf_op jit(solution)/shard_map/all_to_all | solution.py:201
  72.3 27.5 %all-to-all-start.1 = ((f16[16,64,128]{2,1,0:T(8,128)(2,1)}), f16[16,64,128]{2,1,0:T(8,128)(2,1)S(1)}, u32[]{:S(2)}, u32[]{:S(2)}) async-start(f16[16,64,128]{2,1,0:T(8,128)(2,1)} %convert_element_type.34), calls=%async_computation.1 | async-start | bytes 524288 | tf_op jit(solution)/shard_map/all_to_all | solution.py:202
  82.6 17.2 %copy-start.3 = (f32[256,16]{0,1:T(8,128)S(1)}, f32[256,16]{0,1:T(8,128)}, u32[]{:S(2)}) copy-start(f32[256,16]{0,1:T(8,128)} %get-tuple-element.13) | copy-start | bytes 49156
  89.7 12.8 %copy-start.4 = (f32[1024]{0:T(1024)S(1)}, f32[1024]{0:T(1024)}, u32[]{:S(2)}) copy-start(f32[1024]{0:T(1024)} %param.21) | copy-start | bytes 12292
  102.1 2.2 copy-start.7
  171.3 19.1 %copy-start.6 = (f32[1,256,2]{1,2,0:T(2,128)S(1)}, f32[1,256,2]{1,2,0:T(2,128)}, u32[]{:S(2)}) copy-start(f32[1,256,2]{1,2,0:T(2,128)} %param.27) | copy-start | bytes 6148
  182.8 30.2 %all-to-all-start.3 = ((bf16[32,24,1024]{2,1,0:T(8,128)(2,1)}), bf16[32,24,1024]{2,1,0:T(8,128)(2,1)S(1)}, u32[]{:S(2)}, u32[]{:S(2)}) async-start(bf16[32,24,1024]{2,1,0:T(8,128)(2,1)} %bitcast.23), calls=%async_computation.3 | async-start | bytes 3145728 | tf_op jit(solution)/shard_map/all_to_all | solution.py:240
Sparse Core Ops, SparseCore 0:
  25.7 145.5 all-gather.2

commit v2 on v1

--- a/solution.py
+++ b/solution.py
@@ -23,52 +23,54 @@
 
 def pack_weights(gate, up, down):
     moves, row = [], 0
-    for which, piece, step in ((0, gate, FF_BLOCK), (1, up, FF_BLOCK), (2, down, OUT_BLOCK)):
-        for column in range(0, piece.shape[1], step):
+    for which, piece in enumerate((gate, up, down)):
+        for column in range(0, piece.shape[1], FF_BLOCK):
             moves.append((which, column, row, piece.shape[0]))
             row += piece.shape[0]
 
-    def body(gate_ref, up_ref, down_ref, out_ref, sems):
+    def body(gate_ref, up_ref, down_ref, out_ref):
         sources = (gate_ref, up_ref, down_ref)
-        copies = [
-            pltpu.make_async_copy(
-                sources[which].at[:, column : column + FF_BLOCK],
-                out_ref.at[first : first + rows, :],
-                sems.at[i],
-            )
-            for i, (which, column, first, rows) in enumerate(moves)
-        ]
-        for copy in copies:
-            copy.start()
-        for copy in copies:
-            copy.wait()
-
-    anywhere = pl.BlockSpec(memory_space=pl.ANY)
-    return pl.pallas_call(
-        body,
-        in_specs=[anywhere] * 3,
-        out_specs=anywhere,
-        out_shape=jax.ShapeDtypeStruct((row, FF_BLOCK), gate.dtype),
-        scratch_shapes=[pltpu.SemaphoreType.DMA((len(moves),))],
-    )(gate, up, down)
-
-
-def scan_states(received):
-    count, padded, state = received.shape
-    width = padded - HEAD_PAD
-
-    def body(in_ref, out_ref):
-        running = jnp.zeros((width, state), f32)
-        for z in range(count):
-            out_ref[z] = running.astype(out_ref.dtype)
-            if z + 1 < count:
-                tail = in_ref[z, width:padded, :].astype(f32)
-                decay = tail[0:1, :] + (tail[1:2, :] + tail[2:3, :] / SPLIT) / SPLIT
-                running = decay * running + in_ref[z, 0:width, :].astype(f32)
-
-    return pl.pallas_call(
-        body, out_shape=jax.ShapeDtypeStruct((count, width, state), received.dtype)
-    )(received)
+        for which, column, first, rows in moves:
+            out_ref[first : first + rows, :] = sources[which][:, column : column + FF_BLOCK]
+
+    return pl.pallas_call(body, out_shape=jax.ShapeDtypeStruct((row, FF_BLOCK), gate.dtype))(
+        gate, up, down
+    )
+
+
+def incoming_states(local_end, through):
+    heads, width, state = local_end.shape
+    count = lax.axis_size("tm")
+    group = 4
+    groups = [[g * group + m for m in range(group)] for g in range(count // group)]
+    part_a = lax.reduce_precision(through, 5, 10)
+    rest = (through - part_a) * SPLIT
+    part_b = lax.reduce_precision(rest, 5, 10)
+    part_c = (rest - part_b) * SPLIT
+    zero = jnp.zeros_like(through)
+    tail = jnp.stack([part_a, part_b, part_c] + [zero] * (HEAD_PAD - 3), axis=1)
+    tail = jnp.broadcast_to(tail[:, :, None], (heads, HEAD_PAD, state))
+    sent = jnp.concatenate([local_end, tail], axis=1).astype(f16)
+    shared = lax.all_to_all(sent, "tm", 0, 0, tiled=True, axis_index_groups=groups)
+    shared = shared.reshape(group, heads // group, width + HEAD_PAD, state).astype(f32)
+    own = shared[:, :, :width]
+    tail = shared[:, :, width:]
+    decay = tail[:, :, 0:1] + (tail[:, :, 1:2] + tail[:, :, 2:3] / SPLIT) / SPLIT
+
+    total, passed = own[0], decay[0]
+    for m in range(1, group):
+        total = decay[m] * total + own[m]
+        passed = passed * decay[m]
+    entry = jnp.zeros_like(total)
+    for g in range(count // group - 1):
+        hops = [(g * group + m, (g + 1) * group + m) for m in range(group)]
+        handed = lax.ppermute((passed * entry + total).astype(f16), "tm", hops)
+        entry = entry + handed.astype(f32)
+    before = [entry]
+    for m in range(group - 1):
+        before.append(decay[m] * before[-1] + own[m])
+    returned = jnp.concatenate(before, axis=0).astype(f16)
+    return lax.all_to_all(returned, "tm", 0, 0, tiled=True, axis_index_groups=groups).astype(f32)
 
 
 def expert_layer(rows, weights, model_width, hidden_width):
@@ -190,16 +192,7 @@
     remains = jnp.exp(running[-1][None, :] - running)
     local_end = jnp.einsum("jhp,jn->hpn", values * remains[:, :, None], b_rows, precision=exact_mode)
     through = jnp.exp(running[-1])
-    part_a = lax.reduce_precision(through, 5, 10)
-    rest = (through - part_a) * SPLIT
-    part_b = lax.reduce_precision(rest, 5, 10)
-    part_c = (rest - part_b) * SPLIT
-    zero = jnp.zeros_like(through)
-    tail = jnp.stack([part_a, part_b, part_c] + [zero] * (HEAD_PAD - 3), axis=1)
-    tail = jnp.broadcast_to(tail[:, :, None], (heads, HEAD_PAD, b_rows.shape[1]))
-    outgoing_state = jnp.concatenate([local_end, tail], axis=1).astype(f16)
-    by_head = lax.all_to_all(outgoing_state, "tm", 0, 0, tiled=True).astype(f32)
-    incoming = lax.all_to_all(scan_states(by_head).astype(f16), "tm", 0, 0, tiled=True).astype(f32)
+    incoming = incoming_states(local_end, through)
 
     across = running.T[:, :, None] - running.T[:, None, :]
     places = jnp.arange(length)

time: 224 us -> 189 us (0.84)
  Pallas kernels: 35.4 us -> 16.5 us
  waiting for transfers between devices: 84.2 us -> 69.5 us
  starting transfers between devices: 32 us -> 35.3 us
  other arithmetic: 7.4 us -> 4.6 us
    all_to_all x2, waiting for transfers between devices: 29.4 us -> 9.04 us  [the longest x1 5.54 us: incoming_states(): lax.all_to_all(sent, 'tm', 0, 0, tiled=True, axis_index_groups=groups)]
    pallas_call x2 -> x1, Pallas kernels: 20.9 us -> 2.02 us  [pack_weights(): pl.pallas_call(body, out_shape=jax.ShapeDtypeStruct((row, FF_BLOCK), gate...]
    ppermute x0 -> x3, starting transfers between devices: none -> 12.3 us  [incoming_states(): handed = lax.ppermute((passed * entry + total).astype(f16), 'tm', hops)]
    all_to_all x2, starting transfers between devices: 24.4 us -> 13.9 us  [the longest x1 7.48 us: incoming_states(): lax.all_to_all(returned, 'tm', 0, 0, tiled=True, axis_index_groups=groups)]
    all_gather x1, waiting for transfers between devices: 32.3 us -> 36.2 us  [per_device(): lax.all_gather(pack_weights(w_gate[0], w_up[0], w_down[0]), 'tm', axis=0)]
    convert_element_type x2 -> x4, other arithmetic: 2.65 us -> 0.15 us  [the longest x3 0.11 us: incoming_states(): handed = lax.ppermute((passed * entry + total).astype(f16), 'tm', hops)]
  transfers between devices with their start and end apart: 4 -> 7, of which waited for: 4 -> 5; matrix products, arithmetic and copies ran while one was open for 11% -> 11% of each run, Pallas kernels for 1% -> 0%
where the time goes in v2:
time: 189 us; the launch traced here: 188 us
  waiting for transfers between devices  69.5 us (37%)
  starting transfers between devices  35.3 us (19%)
  blocking collectives  32.1 us (17%)
  Pallas kernels  16.5 us (9%)
  between operations  13.7 us (7%)
  matrix products  10.7 us (6%)
  local copies, waits for them, and re-layouts  5.5 us (3%)
  other arithmetic  4.6 us (2%)
    all_gather x1, waiting for transfers between devices, per_device(): lax.all_gather(pack_weights(w_gate[0], w_up[0], w_down[0]), 'tm', axis=0)  36.2 us
    all_to_all x1, blocking collectives, per_device(): lax.all_to_all(outgoing.reshape(experts, capacity, model_width), 'expert'...  32.1 us
    all_to_all x1, waiting for transfers between devices, per_device(): lax.all_to_all(produced.reshape(experts, capacity, model_width), 'expert'...  22.5 us
    ppermute x3, starting transfers between devices, incoming_states(): handed = lax.ppermute((passed * entry + total).astype(f16), 'tm', hops)  12.3 us
    pallas_call x1, Pallas kernels, expert_layer(): pl.pallas_call(body, grid=(ff_steps + out_steps,), in_specs=[pl.BlockSpec...  11.5 us
    all_to_all x1, starting transfers between devices, per_device(): lax.all_to_all(produced.reshape(experts, capacity, model_width), 'expert'...  9.04 us
    all_to_all x1, starting transfers between devices, incoming_states(): lax.all_to_all(returned, 'tm', 0, 0, tiled=True, axis_index_groups=groups)  7.48 us
    all_to_all x1, starting transfers between devices, incoming_states(): lax.all_to_all(sent, 'tm', 0, 0, tiled=True, axis_index_groups=groups)  6.44 us
  transfers between devices with their start and end apart: 7, of which 5 were waited for; matrix products, arithmetic and copies ran while one was open for 11% of the time, Pallas kernels for 0%

profile of v2, /device:TPU:1, one launch (start us, length us, event | category | flops | bytes accessed | tf_op | source)
XLA Modules:
  0.0 187.9 jit_solution(11683561857213457782)
XLA Ops:
  6.5 2.0 %shard_map.136 = bf16[576,512]{1,0:T(8,128)(2,1)} custom-call(bf16[64,1536]{1,0:T(8,128)(2,1)} %bitcast.175, bf16[64,1536]{1,0:T(8,128)(2,1)} %bitcast.176, bf16[96,1024]{1,0:T(8,128)(2,1)} %bitcast.177), custom_call_target="tpu_custom_call" | custom-call | tf_op jit(solution)/shard_map/pallas_call | solution.py:36
  8.6 0.0 all-gather.3.cloned.1.call-update
  8.6 0.7 copy_bitcast_fusion.1
  9.3 0.6 reduce-window.6
  9.9 0.2 slice_reduce_fusion.4
  10.1 0.1 fusion.49
  10.2 0.2 slice_reduce_fusion.5
  10.4 0.1 copy.100
  10.5 0.1 copy.101
  10.6 0.1 copy.102
  10.6 0.1 stack.10
  10.7 1.6 copy.98
  12.3 0.1 bitcast_exponential_fusion
  12.4 0.0 copy-start.1
  12.4 0.1 bitcast_multiply_fusion.1
  12.5 1.0 convolution_convert_fusion.1
  13.5 0.1 broadcast_in_dim.34
  13.6 0.8 pad_maximum_fusion
  14.4 6.4 %all-to-all-start = ((f16[16,72,128]{2,1,0:T(8,128)(2,1)}), f16[16,72,128]{2,1,0:T(8,128)(2,1)S(1)}, u32[]{:S(2)}, u32[]{:S(2)}) async-start(f16[16,72,128]{2,1,0:T(8,128)(2,1)} %pad_maximum_fusion), calls=%async_computation | async-start | bytes 589824 | tf_op jit(solution)/shard_map/all_to_all | solution.py:54
  20.8 0.1 copy.93
  21.0 0.2 slice_reduce_fusion.3
  21.2 5.5 %all-to-all-done = f16[16,72,128]{2,1,0:T(8,128)(2,1)S(1)} async-done(((f16[16,72,128]{2,1,0:T(8,128)(2,1)}), f16[16,72,128]{2,1,0:T(8,128)(2,1)S(1)}, u32[]{:S(2)}, u32[]{:S(2)}) %all-to-all-start) | async-done | bytes 294944 | tf_op jit(solution)/shard_map/all_to_all | solution.py:54
  26.9 11.0 %collective-permute-start = (f16[4,64,128]{2,1,0:T(8,128)(2,1)S(1)}, f16[4,64,128]{2,1,0:T(8,128)(2,1)S(1)}, u32[]{:S(2)}, u32[]{:S(2)}) collective-permute-start(f16[4,64,128]{2,1,0:T(8,128)(2,1)S(1)} %get-tuple-element.15), channel_id=1, source_target_pairs={{0,128},{32,160},{64,192},{96,224},{1,129},{33,161},{65,193},{97,2... | collective-permute-start | bytes 196616 | tf_op jit(solution)/shard_map/ppermute | solution.py:67
  37.9 0.3 convolution_convert_fusion.2
  38.2 0.1 copy.94
  38.2 1.7 collective-permute-done
  40.0 0.7 collective-permute-start.1
  40.7 0.1 copy.95
  40.9 0.7 collective-permute-start.2
  41.6 1.2 copy.107
  42.8 0.1 fusion.51
  42.9 0.8 pad_maximum_fusion.1
  43.7 7.5 %all-to-all-start.1 = ((f16[16,64,128]{2,1,0:T(8,128)(2,1)}), f16[16,64,128]{2,1,0:T(8,128)(2,1)S(1)}, u32[]{:S(2)}, u32[]{:S(2)}) async-start(f16[16,64,128]{2,1,0:T(8,128)(2,1)} %pad_maximum_fusion.1), calls=%async_computation.1 | async-start | bytes 524288 | tf_op jit(solution)/shard_map/all_to_all | solution.py:73
  51.2 0.2 slice_reduce_fusion.1
  51.4 0.4 fusion.37
  51.8 6.1 %fusion.16 = f32[256,16,64]{0,2,1:T(8,128)} fusion(f32[256,16,64]{0,2,1:T(8,128)S(1)} %bitcast.167, f32[256,256]{1,0:T(8,128)S(1)} %fusion.37, f32[16,256]{1,0:T(8,128)S(1)} %get-tuple-element.28, pred[256,256]{1,0:T(8,128)(4,1)S(1)} %iota_compare_fusion.3, f32[16]{0:T(128)S(1)} %copy-done.8), kind=kOutput, calls=%fused_computation.16 | convolution fusion | flops 810024960 | bytes 2441280 | tf_op jit(solution)/shard_map/hij,jhp->ihp/dot_general | solution.py:202
  58.0 3.5 %all-to-all-done.1 = f16[16,64,128]{2,1,0:T(8,128)(2,1)S(1)} async-done(((f16[16,64,128]{2,1,0:T(8,128)(2,1)}), f16[16,64,128]{2,1,0:T(8,128)(2,1)S(1)}, u32[]{:S(2)}, u32[]{:S(2)}) %all-to-all-start.1) | async-done | bytes 262176 | tf_op jit(solution)/shard_map/all_to_all | solution.py:73
  61.5 2.3 %multiply_reduce_fusion.1 = (f32[256]{0:T(256)S(1)}, f32[256,16,64]{0,2,1:T(8,128)S(1)}) fusion(f32[256,16,64]{0,2,1:T(8,128)S(1)} %bitcast.173, f32[256,16,64]{0,2,1:T(8,128)} %fusion.16, f16[16,64,128]{2,1,0:T(8,128)(2,1)S(1)} %all-to-all-done.1, f32[1,256,128]{2,1,0:T(8,128)S(1)} %copy-done, f32[256,16]{0,1:T(8,128)S(1)} %get-tuple-element.25), kind=kOutput, calls=%fused_computation.31 | convolution fusion | flops 405012224 | bytes 3556352 | tf_op jit(solution)/shard_map/in,hpn->ihp/dot_general | solution.py:205
  63.8 0.3 copy.106
  64.1 1.8 multiply_reduce_fusion
  65.9 0.7 convolution_convert_fusion
  66.6 32.1 %all_to_all.20 = bf16[32,24,1024]{2,1,0:T(8,128)(2,1)S(1)} all-to-all(bf16[32,24,1024]{2,1,0:T(8,128)(2,1)S(1)} %bitcast.171), channel_id=1, replica_groups=mesh['tm'=16,'expert'=32] {'expert'}, dimensions={0} | all-to-all | bytes 3145728 | tf_op jit(solution)/shard_map/all_to_all | solution.py:227
  98.7 36.2 %all-gather.3.cloned.1.call-done = bf16[9216,512]{1,0:T(8,128)(2,1)} async-done(((bf16[576,512]{1,0:T(8,128)(2,1)}), bf16[9216,512]{1,0:T(8,128)(2,1)}) %all-gather.3.cloned.1.call-update) | async-done | bytes 9437200 | tf_op jit(solution)/shard_map/all_gather | solution.py:185
  134.9 11.5 %shard_map.137 = bf16[768,1024]{1,0:T(8,128)(2,1)} custom-call(bf16[768,1024]{1,0:T(8,128)(2,1)S(1)} %bitcast.162, bf16[16,576,512]{2,1,0:T(8,128)(2,1)} %bitcast.164, bf16[16,576,512]{2,1,0:T(8,128)(2,1)} %bitcast.165, bf16[16,576,512]{2,1,0:T(8,128)(2,1)} %bitcast.166), custom_call_target="tpu_custom_call" | custom-call | tf_op jit(solution)/shard_map/pallas_call | solution.py:110
  146.4 9.0 %all-to-all-start.3 = ((bf16[32,24,1024]{2,1,0:T(8,128)(2,1)}), bf16[32,24,1024]{2,1,0:T(8,128)(2,1)S(1)}, u32[]{:S(2)}, u32[]{:S(2)}) async-start(bf16[32,24,1024]{2,1,0:T(8,128)(2,1)} %bitcast.33), calls=%async_computation.3 | async-start | bytes 3145728 | tf_op jit(solution)/shard_map/all_to_all | solution.py:233
  155.4 0.1 copy.108
  155.6 22.5 %all-to-all-done.3 = bf16[32,24,1024]{2,1,0:T(8,128)(2,1)S(1)} async-done(((bf16[32,24,1024]{2,1,0:T(8,128)(2,1)}), bf16[32,24,1024]{2,1,0:T(8,128)(2,1)S(1)}, u32[]{:S(2)}, u32[]{:S(2)}) %all-to-all-start.3) | async-done | bytes 1572896 | tf_op jit(solution)/shard_map/all_to_all | solution.py:233
  178.1 3.0 %shard_map.138 = f32[256,1024]{1,0:T(8,128)} custom-call(bf16[768,1024]{1,0:T(8,128)(2,1)S(1)} %bitcast.161, f32[256,1024]{1,0:T(8,128)S(1)} %get-tuple-element.12.hres_ref, s32[256,2]{1,0:T(8,128)S(1)} %multiply_add_fusion.2.target_ref, f32[256,2]{1,0:T(8,128)S(1)} %bitcast.163), custom_call_target="tpu_custom_call" | custom-call | tf_op jit(solution)/shard_map/pallas_call | solution.py:146
  (40 shorter events, 0.5 us)
Async XLA Ops:
  6.5 44.9 %copy-start = (f32[1,256,128]{2,1,0:T(8,128)S(1)}, f32[1,256,128]{2,1,0:T(8,128)}, u32[]{:S(2)}) copy-start(f32[1,256,128]{2,1,0:T(8,128)} %param.17) | copy-start | bytes 393220
  6.5 6.0 %copy-start.3 = (f32[1,256,128]{2,1,0:T(8,128)S(1)}, f32[1,256,128]{2,1,0:T(8,128)}, u32[]{:S(2)}) copy-start(f32[1,256,128]{2,1,0:T(8,128)} %param.16) | copy-start | bytes 393220
  6.5 128.3 %all-gather.3.cloned.1.call-start = ((), (), s32[]{:S(2)}) async-start(), calls=%async_computation.4 | async-start | bytes 10027008 | tf_op jit(solution)/shard_map/all_gather | solution.py:185
  6.5 14.3 %copy-start.5 = (s32[1,256,2]{1,2,0:T(2,128)S(1)}, s32[1,256,2]{1,2,0:T(2,128)}, u32[]{:S(2)}) copy-start(s32[1,256,2]{1,2,0:T(2,128)} %param.26) | copy-start | bytes 6148
  12.4 29.2 %copy-start.1 = (bf16[1,256,1024]{2,1,0:T(8,128)(2,1)S(1)}, bf16[1,256,1024]{2,1,0:T(8,128)(2,1)}, u32[]{:S(2)}) copy-start(bf16[1,256,1024]{2,1,0:T(8,128)(2,1)} %param.15) | copy-start | bytes 1572868
  14.4 12.3 %all-to-all-start = ((f16[16,72,128]{2,1,0:T(8,128)(2,1)}), f16[16,72,128]{2,1,0:T(8,128)(2,1)S(1)}, u32[]{:S(2)}, u32[]{:S(2)}) async-start(f16[16,72,128]{2,1,0:T(8,128)(2,1)} %pad_maximum_fusion), calls=%async_computation | async-start | bytes 589824 | tf_op jit(solution)/shard_map/all_to_all | solution.py:54
  20.8 31.0 %copy-start.8 = (f32[16]{0:T(128)S(1)}, f32[16]{0:T(128)}, u32[]{:S(2)}) copy-start(f32[16]{0:T(128)} %param.19) | copy-start | bytes 196
  26.9 13.1 %collective-permute-start = (f16[4,64,128]{2,1,0:T(8,128)(2,1)S(1)}, f16[4,64,128]{2,1,0:T(8,128)(2,1)S(1)}, u32[]{:S(2)}, u32[]{:S(2)}) collective-permute-start(f16[4,64,128]{2,1,0:T(8,128)(2,1)S(1)} %get-tuple-element.15), channel_id=1, source_target_pairs={{0,128},{32,160},{64,192},{96,224},{1,129},{33,161},{65,193},{97,2... | collective-permute-start | bytes 196616 | tf_op jit(solution)/shard_map/ppermute | solution.py:67
  40.0 0.8 collective-permute-start.1
  40.9 1.9 %collective-permute-start.2 = (f16[4,64,128]{2,1,0:T(8,128)(2,1)S(1)}, f16[4,64,128]{2,1,0:T(8,128)(2,1)S(1)}, u32[]{:S(2)}, u32[]{:S(2)}) collective-permute-start(f16[4,64,128]{2,1,0:T(8,128)(2,1)S(1)} %add_convert_fusion.1), channel_id=1, source_target_pairs={{256,384},{288,416},{320,448},{352,480},{257,385},{289,417},{321,4... | collective-permute-start | bytes 196616 | tf_op jit(solution)/shard_map/ppermute | solution.py:67
  43.7 17.8 %all-to-all-start.1 = ((f16[16,64,128]{2,1,0:T(8,128)(2,1)}), f16[16,64,128]{2,1,0:T(8,128)(2,1)S(1)}, u32[]{:S(2)}, u32[]{:S(2)}) async-start(f16[16,64,128]{2,1,0:T(8,128)(2,1)} %pad_maximum_fusion.1), calls=%async_computation.1 | async-start | bytes 524288 | tf_op jit(solution)/shard_map/all_to_all | solution.py:73
  51.8 9.7 %copy-start.2 = (f32[1,256,1024]{1,2,0:T(8,128)S(1)}, f32[1,256,1024]{1,2,0:T(8,128)}, u32[]{:S(2)}) copy-start(f32[1,256,1024]{1,2,0:T(8,128)} %copy.107) | copy-start | bytes 3145732
  58.0 6.2 %copy-start.4 = (f32[1024]{0:T(1024)S(1)}, f32[1024]{0:T(1024)}, u32[]{:S(2)}) copy-start(f32[1024]{0:T(1024)} %param.21) | copy-start | bytes 12292
  63.8 2.1 %copy-start.7 = (f32[1024]{0:T(1024)S(1)}, f32[1024]{0:T(1024)}, u32[]{:S(2)}) copy-start(f32[1024]{0:T(1024)} %param.22) | copy-start | bytes 12292
  134.9 20.6 %copy-start.6 = (f32[1,256,2]{1,2,0:T(2,128)S(1)}, f32[1,256,2]{1,2,0:T(2,128)}, u32[]{:S(2)}) copy-start(f32[1,256,2]{1,2,0:T(2,128)} %param.27) | copy-start | bytes 6148
  146.4 31.7 %all-to-all-start.3 = ((bf16[32,24,1024]{2,1,0:T(8,128)(2,1)}), bf16[32,24,1024]{2,1,0:T(8,128)(2,1)S(1)}, u32[]{:S(2)}, u32[]{:S(2)}) async-start(bf16[32,24,1024]{2,1,0:T(8,128)(2,1)} %bitcast.33), calls=%async_computation.3 | async-start | bytes 3145728 | tf_op jit(solution)/shard_map/all_to_all | solution.py:233
Sparse Core Ops, SparseCore 0:
  9.4 125.3 all-gather.2

commit v3 on v2

--- a/solution.py
+++ b/solution.py
@@ -14,7 +14,6 @@
 HEAD_PAD = 8
 SPLIT = 2048.0
 FF_BLOCK = 512
-OUT_BLOCK = 512
 
 
 def rms_scale(rows, gain):
@@ -75,88 +74,112 @@
 
 def expert_layer(rows, weights, model_width, hidden_width):
     total = rows.shape[0]
-    parts = weights.shape[0]
+    parts, packed, _ = weights.shape
     k_rows = model_width // parts
     f_rows = hidden_width // parts
     ff_steps = hidden_width // FF_BLOCK
-    out_steps = model_width // OUT_BLOCK
-    down_first = (2 * ff_steps * k_rows) // f_rows
-    row_block = 256
-
-    def body(x_ref, g_ref, u_ref, d_ref, out_ref, hid_ref):
-        step = pl.program_id(0)
+    out_steps = model_width // FF_BLOCK
+    blocks = [(k_rows * i, k_rows) for i in range(2 * ff_steps)]
+    blocks += [(2 * ff_steps * k_rows + f_rows * i, f_rows) for i in range(out_steps)]
+    down = list(range(2 * ff_steps, len(blocks)))
+    order = [b for f in range(ff_steps) for b in (f, ff_steps + f)] + down
+    out_rows = total // 3
+
+    def body(x_ref, w_ref, out_ref, w_buf, hid_ref, out_buf, w_sems, out_sems):
+        def copy(block, part):
+            first, count = blocks[block]
+            return pltpu.make_async_copy(
+                w_ref.at[part, first : first + count, :],
+                w_buf.at[part, first : first + count, :],
+                w_sems.at[block, part],
+            )
+
+        for block in order:
+            for part in range(parts):
+                copy(block, part).start()
+
+        def matrix(block):
+            first, count = blocks[block]
+            for part in range(parts):
+                copy(block, part).wait()
+            return w_buf[:, first : first + count, :].reshape(parts * count, FF_BLOCK)
+
         for f in range(ff_steps):
-
-            @pl.when(step == f)
-            def _(f=f):
-                wg = g_ref[...].reshape(model_width, FF_BLOCK)
-                wu = u_ref[...].reshape(model_width, FF_BLOCK)
-                for r in range(0, total, row_block):
-                    x = x_ref[r : r + row_block, :]
-                    gate = jnp.dot(x, wg, preferred_element_type=f32)
-                    upper = jnp.dot(x, wu, preferred_element_type=f32)
-                    hidden = (gate / (1.0 + jnp.exp(-gate))) * upper
-                    hid_ref[r : r + row_block, f * FF_BLOCK : (f + 1) * FF_BLOCK] = hidden.astype(bf16)
-
-        @pl.when(step >= ff_steps)
-        def _():
-            wd = d_ref[...].reshape(hidden_width, OUT_BLOCK)
-            for r in range(0, total, row_block):
-                out_ref[r : r + row_block, :] = jnp.dot(
-                    hid_ref[r : r + row_block, :], wd, preferred_element_type=f32
+            x = x_ref[...]
+            gate = jnp.dot(x, matrix(f), preferred_element_type=f32)
+            upper = jnp.dot(x, matrix(ff_steps + f), preferred_element_type=f32)
+            hidden = (gate / (1.0 + jnp.exp(-gate))) * upper
+            hid_ref[:, f * FF_BLOCK : (f + 1) * FF_BLOCK] = hidden.astype(bf16)
+        sides = [matrix(block) for block in down]
+        leaving = []
+        for i, r in enumerate(range(0, total, out_rows)):
+            for n, side in enumerate(sides):
+                out_buf[r : r + out_rows, n * FF_BLOCK : (n + 1) * FF_BLOCK] = jnp.dot(
+                    hid_ref[r : r + out_rows, :], side, preferred_element_type=f32
                 ).astype(bf16)
-
-    last = ff_steps - 1
+            leaving.append(
+                pltpu.make_async_copy(
+                    out_buf.at[r : r + out_rows, :], out_ref.at[r : r + out_rows, :], out_sems.at[i]
+                )
+            )
+            leaving[-1].start()
+        for each in leaving:
+            each.wait()
+
+    anywhere = pl.BlockSpec(memory_space=pl.ANY)
     return pl.pallas_call(
         body,
-        grid=(ff_steps + out_steps,),
-        in_specs=[
-            pl.BlockSpec((total, model_width), lambda i: (0, 0)),
-            pl.BlockSpec((parts, k_rows, FF_BLOCK), lambda i: (0, jnp.minimum(i, last), 0)),
-            pl.BlockSpec((parts, k_rows, FF_BLOCK), lambda i: (0, ff_steps + jnp.minimum(i, last), 0)),
-            pl.BlockSpec(
-                (parts, f_rows, OUT_BLOCK),
-                lambda i: (0, down_first + jnp.maximum(i - ff_steps, 0), 0),
-            ),
+        in_specs=[pl.BlockSpec(memory_space=pltpu.VMEM), anywhere],
+        out_specs=anywhere,
+        out_shape=jax.ShapeDtypeStruct((total, model_width), bf16),
+        scratch_shapes=[
+            pltpu.VMEM((parts, packed, FF_BLOCK), bf16),
+            pltpu.VMEM((total, hidden_width), bf16),
+            pltpu.VMEM((total, model_width), bf16),
+            pltpu.SemaphoreType.DMA((len(blocks), parts)),
+            pltpu.SemaphoreType.DMA((3,)),
         ],
-        out_specs=pl.BlockSpec((total, OUT_BLOCK), lambda i: (0, jnp.maximum(i - ff_steps, 0))),
-        out_shape=jax.ShapeDtypeStruct((total, model_width), bf16),
-        scratch_shapes=[pltpu.VMEM((total, hidden_width), bf16)],
-        compiler_params=pltpu.CompilerParams(vmem_limit_bytes=40 * MIB),
-    )(rows, *[pltpu.with_memory_space_constraint(weights, pltpu.HBM)] * 3)
-
-
-def combine(back, hres, targets, route_weights):
-    slots, model_width = back.shape
-    length = hres.shape[0]
+        compiler_params=pltpu.CompilerParams(vmem_limit_bytes=32 * MIB),
+    )(rows, pltpu.with_memory_space_constraint(weights, pltpu.HBM))
+
+
+def combine(back, hres, selection, route_weights):
+    length, model_width = hres.shape
     block = 256
-
-    def body(back_ref, hres_ref, target_ref, weight_ref, out_ref, sel_ref):
-        @pl.when(pl.program_id(0) == 0)
-        def _():
-            places = lax.broadcasted_iota(jnp.int32, (length, slots), 1)
-            for k in range(2):
-                sel_ref[k] = jnp.where(target_ref[:, k : k + 1] == places, 1.0, 0.0).astype(bf16)
-
-        back_block = back_ref[...]
-        first = jnp.dot(sel_ref[0], back_block, preferred_element_type=f32)
-        second = jnp.dot(sel_ref[1], back_block, preferred_element_type=f32)
-        out_ref[...] = hres_ref[...] + (weight_ref[:, 0:1] * first + weight_ref[:, 1:2] * second)
+    steps = model_width // block
+
+    def body(back_ref, hres_ref, sel_ref, weight_in, out_ref, out_buf, weight_ref, sems):
+        arriving = pltpu.make_async_copy(weight_in, weight_ref, sems.at[steps])
+        arriving.start()
+        leaving = []
+        for i in range(steps):
+            part = slice(i * block, (i + 1) * block)
+            rows = back_ref[:, part]
+            first = jnp.dot(sel_ref[0], rows, preferred_element_type=f32)
+            second = jnp.dot(sel_ref[1], rows, preferred_element_type=f32)
+            if i == 0:
+                arriving.wait()
+                weight_a, weight_b = weight_ref[:, 0:1], weight_ref[:, 1:2]
+            out_buf[:, part] = hres_ref[:, part] + (weight_a * first + weight_b * second)
+            leaving.append(
+                pltpu.make_async_copy(out_buf.at[:, part], out_ref.at[:, part], sems.at[i])
+            )
+            leaving[-1].start()
+        for each in leaving:
+            each.wait()
 
     return pl.pallas_call(
         body,
-        grid=(model_width // block,),
-        in_specs=[
-            pl.BlockSpec((slots, block), lambda i: (0, i)),
-            pl.BlockSpec((length, block), lambda i: (0, i)),
-            pl.BlockSpec((length, 2), lambda i: (0, 0)),
-            pl.BlockSpec((length, 2), lambda i: (0, 0)),
+        in_specs=[pl.BlockSpec(memory_space=pltpu.VMEM)] * 3 + [pl.BlockSpec(memory_space=pl.ANY)],
+        out_specs=pl.BlockSpec(memory_space=pl.ANY),
+        out_shape=jax.ShapeDtypeStruct((length, model_width), f32),
+        scratch_shapes=[
+            pltpu.VMEM((length, model_width), f32),
+            pltpu.VMEM(route_weights.shape, f32),
+            pltpu.SemaphoreType.DMA((steps + 1,)),
         ],
-        out_specs=pl.BlockSpec((length, block), lambda i: (0, i)),
-        out_shape=jax.ShapeDtypeStruct((length, model_width), f32),
-        scratch_shapes=[pltpu.VMEM((2, length, slots), bf16)],
-        compiler_params=pltpu.CompilerParams(vmem_limit_bytes=32 * MIB),
-    )(back, hres, targets, route_weights)
+        compiler_params=pltpu.CompilerParams(vmem_limit_bytes=16 * MIB),
+    )(back, hres, selection, route_weights)
 
 
 def per_device(
@@ -223,6 +246,9 @@
     spread = (
         (targets[:, 0][None, :] == slot_ids[:, None]) | (targets[:, 1][None, :] == slot_ids[:, None])
     ).astype(bf16)
+    selection = jnp.stack(
+        [targets[:, k : k + 1] == slot_ids[None, :] for k in range(targets.shape[1])]
+    ).astype(bf16)
     outgoing = jnp.dot(spread, normed, preferred_element_type=f32).astype(bf16)
     received = lax.all_to_all(
         outgoing.reshape(experts, capacity, model_width), "expert", 0, 0, tiled=True
@@ -233,7 +259,7 @@
     back = lax.all_to_all(
         produced.reshape(experts, capacity, model_width), "expert", 0, 0, tiled=True
     )
-    out = combine(back.reshape(experts * capacity, model_width), hres, targets, route_weights[0])
+    out = combine(back.reshape(experts * capacity, model_width), hres, selection, route_weights[0])
     return out.reshape(1, length, model_width)
 
 

time: 189 us -> 190 us (level)
  waiting for transfers between devices: 69.5 us -> 67 us
  local copies, waits for them, and re-layouts: 5.5 us -> 7.65 us
    all_gather x1, waiting for transfers between devices: 36.2 us -> 34 us  [per_device(): lax.all_gather(pack_weights(w_gate[0], w_up[0], w_down[0]), 'tm', axis=0)]
  transfers between devices with their start and end apart: 7 -> 7, of which waited for: 5 -> 5; matrix products, arithmetic and copies ran while one was open for 11% -> 12% of each run, Pallas kernels for 0% -> 0%
where the time goes in v3:
time: 190 us; the launch traced here: 189 us
  waiting for transfers between devices  67 us (35%)
  starting transfers between devices  35.3 us (19%)
  blocking collectives  32.2 us (17%)
  Pallas kernels  16.8 us (9%)
  between operations  13.7 us (7%)
  matrix products  11.7 us (6%)
  local copies, waits for them, and re-layouts  7.65 us (4%)
  other arithmetic  4.96 us (3%)
    all_gather x1, waiting for transfers between devices, per_device(): lax.all_gather(pack_weights(w_gate[0], w_up[0], w_down[0]), 'tm', axis=0)  34 us
    all_to_all x1, blocking collectives, per_device(): lax.all_to_all(outgoing.reshape(experts, capacity, model_width), 'expert'...  32.2 us
    all_to_all x1, waiting for transfers between devices, per_device(): lax.all_to_all(produced.reshape(experts, capacity, model_width), 'expert'...  21.5 us
    pallas_call x1, Pallas kernels, expert_layer(): pl.pallas_call(body, in_specs=[pl.BlockSpec(memory_space=pltpu.VMEM), any...  12.8 us
    ppermute x3, starting transfers between devices, incoming_states(): handed = lax.ppermute((passed * entry + total).astype(f16), 'tm', hops)  12.3 us
    all_to_all x1, starting transfers between devices, per_device(): lax.all_to_all(produced.reshape(experts, capacity, model_width), 'expert'...  9.16 us
    all_to_all x1, starting transfers between devices, incoming_states(): lax.all_to_all(returned, 'tm', 0, 0, tiled=True, axis_index_groups=groups)  7.35 us
    all_to_all x1, starting transfers between devices, incoming_states(): lax.all_to_all(sent, 'tm', 0, 0, tiled=True, axis_index_groups=groups)  6.44 us
  transfers between devices with their start and end apart: 7, of which 5 were waited for; matrix products, arithmetic and copies ran while one was open for 12% of the time, Pallas kernels for 0%

profile of v3, /device:TPU:1, one launch (start us, length us, event | category | flops | bytes accessed | tf_op | source)
XLA Modules:
  0.0 189.3 jit_solution(15799881668116758987)
XLA Ops:
  6.5 2.0 %shard_map.136 = bf16[576,512]{1,0:T(8,128)(2,1)} custom-call(bf16[64,1536]{1,0:T(8,128)(2,1)} %bitcast.175, bf16[64,1536]{1,0:T(8,128)(2,1)} %bitcast.176, bf16[96,1024]{1,0:T(8,128)(2,1)} %bitcast.177), custom_call_target="tpu_custom_call" | custom-call | tf_op jit(solution)/shard_map/pallas_call | solution.py:35
  8.6 0.0 all-gather.3.cloned.1.call-update
  8.6 0.7 copy_bitcast_fusion.1
  9.3 0.6 reduce-window.6
  9.9 0.2 slice_reduce_fusion
  10.1 0.1 fusion.49
  10.2 0.2 slice_reduce_fusion.1
  10.4 0.1 copy.91
  10.5 0.1 copy.92
  10.6 0.1 copy.93
  10.6 0.1 stack.7
  10.7 0.0 copy-start.2
  10.7 1.6 copy.89
  12.4 0.1 bitcast_exponential_fusion
  12.4 0.1 bitcast_multiply_fusion.1
  12.5 1.0 convolution_convert_fusion.1
  13.5 0.0 copy-start.9
  13.6 0.1 broadcast_in_dim.34
  13.6 0.8 pad_maximum_fusion
  14.4 6.4 %all-to-all-start = ((f16[16,72,128]{2,1,0:T(8,128)(2,1)}), f16[16,72,128]{2,1,0:T(8,128)(2,1)S(1)}, u32[]{:S(2)}, u32[]{:S(2)}) async-start(f16[16,72,128]{2,1,0:T(8,128)(2,1)} %pad_maximum_fusion), calls=%async_computation | async-start | bytes 589824 | tf_op jit(solution)/shard_map/all_to_all | solution.py:53
  20.9 0.3 convolution_convert_fusion.2
  21.2 5.6 %all-to-all-done = f16[16,72,128]{2,1,0:T(8,128)(2,1)S(1)} async-done(((f16[16,72,128]{2,1,0:T(8,128)(2,1)}), f16[16,72,128]{2,1,0:T(8,128)(2,1)S(1)}, u32[]{:S(2)}, u32[]{:S(2)}) %all-to-all-start) | async-done | bytes 294944 | tf_op jit(solution)/shard_map/all_to_all | solution.py:53
  26.9 0.1 add_convert_fusion.3
  26.9 11.0 %collective-permute-start = (f16[4,64,128]{2,1,0:T(8,128)(2,1)S(1)}, f16[4,64,128]{2,1,0:T(8,128)(2,1)S(1)}, u32[]{:S(2)}, u32[]{:S(2)}) collective-permute-start(f16[4,64,128]{2,1,0:T(8,128)(2,1)S(1)} %get-tuple-element.11), channel_id=1, source_target_pairs={{0,128},{32,160},{64,192},{96,224},{1,129},{33,161},{65,193},{97,2... | collective-permute-start | bytes 196616 | tf_op jit(solution)/shard_map/ppermute | solution.py:66
  37.9 2.1 %collective-permute-done = f16[4,64,128]{2,1,0:T(8,128)(2,1)S(1)} collective-permute-done((f16[4,64,128]{2,1,0:T(8,128)(2,1)S(1)}, f16[4,64,128]{2,1,0:T(8,128)(2,1)S(1)}, u32[]{:S(2)}, u32[]{:S(2)}) %collective-permute-start) | collective-permute-done | bytes 65568 | tf_op jit(solution)/shard_map/ppermute | solution.py:66
  40.1 0.7 collective-permute-start.1
  40.8 1.2 copy.98
  42.0 0.7 collective-permute-start.2
  42.7 0.1 fusion.51
  42.8 0.8 pad_maximum_fusion.1
  43.6 7.3 %all-to-all-start.1 = ((f16[16,64,128]{2,1,0:T(8,128)(2,1)}), f16[16,64,128]{2,1,0:T(8,128)(2,1)S(1)}, u32[]{:S(2)}, u32[]{:S(2)}) async-start(f16[16,64,128]{2,1,0:T(8,128)(2,1)} %pad_maximum_fusion.1), calls=%async_computation.1 | async-start | bytes 524288 | tf_op jit(solution)/shard_map/all_to_all | solution.py:72
  51.0 0.4 fusion.37
  51.4 6.1 %fusion.16 = f32[256,16,64]{0,2,1:T(8,128)} fusion(f32[256,16,64]{0,2,1:T(8,128)S(1)} %bitcast.169, f32[256,256]{1,0:T(8,128)S(1)} %fusion.37, f32[16,256]{1,0:T(8,128)S(1)} %get-tuple-element.24, pred[256,256]{1,0:T(8,128)(4,1)S(1)} %iota_compare_fusion.5, f32[16]{0:T(128)S(1)} %copy-done.9), kind=kOutput, calls=%fused_computation.17 | convolution fusion | flops 810024960 | bytes 2441280 | tf_op jit(solution)/shard_map/hij,jhp->ihp/dot_general | solution.py:225
  57.5 3.7 %all-to-all-done.1 = f16[16,64,128]{2,1,0:T(8,128)(2,1)S(1)} async-done(((f16[16,64,128]{2,1,0:T(8,128)(2,1)}), f16[16,64,128]{2,1,0:T(8,128)(2,1)S(1)}, u32[]{:S(2)}, u32[]{:S(2)}) %all-to-all-start.1) | async-done | bytes 262176 | tf_op jit(solution)/shard_map/all_to_all | solution.py:72
  61.3 3.2 %multiply_reduce_fusion.1 = (f32[256]{0:T(256)S(1)}, f32[256,16,64]{0,2,1:T(8,128)}) fusion(f32[256,16,64]{0,2,1:T(8,128)S(1)} %bitcast.173, f32[256,16,64]{0,2,1:T(8,128)} %fusion.16, f16[16,64,128]{2,1,0:T(8,128)(2,1)S(1)} %all-to-all-done.1, f32[1,256,128]{2,1,0:T(8,128)S(1)} %copy-done, f32[256,16]{0,1:T(8,128)S(1)} %get-tuple-element.21), kind=kOutput, calls=%fused_computation.32 | convolution fusion | flops 405012224 | bytes 3556352 | tf_op jit(solution)/shard_map/in,hpn->ihp/dot_general | solution.py:228
  64.5 1.6 copy.97
  66.1 1.8 multiply_reduce_fusion
  67.9 0.7 convolution_convert_fusion
  68.6 32.2 %all_to_all.20 = bf16[32,24,1024]{2,1,0:T(8,128)(2,1)S(1)} all-to-all(bf16[32,24,1024]{2,1,0:T(8,128)(2,1)S(1)} %bitcast.171), channel_id=1, replica_groups=mesh['tm'=16,'expert'=32] {'expert'}, dimensions={0} | all-to-all | bytes 3145728 | tf_op jit(solution)/shard_map/all_to_all | solution.py:253
  100.8 34.0 %all-gather.3.cloned.1.call-done = bf16[9216,512]{1,0:T(8,128)(2,1)} async-done(((bf16[576,512]{1,0:T(8,128)(2,1)}), bf16[9216,512]{1,0:T(8,128)(2,1)}) %all-gather.3.cloned.1.call-update) | async-done | bytes 9437200 | tf_op jit(solution)/shard_map/all_gather | solution.py:208
  134.8 12.8 %shard_map.137 = bf16[768,1024]{1,0:T(8,128)(2,1)} custom-call(bf16[768,1024]{1,0:T(8,128)(2,1)S(1)} %bitcast.166, bf16[16,576,512]{2,1,0:T(8,128)(2,1)} %bitcast.168), custom_call_target="tpu_custom_call" | custom-call | tf_op jit(solution)/shard_map/pallas_call | solution.py:130
  147.6 9.2 %all-to-all-start.3 = ((bf16[32,24,1024]{2,1,0:T(8,128)(2,1)}), bf16[32,24,1024]{2,1,0:T(8,128)(2,1)S(1)}, u32[]{:S(2)}, u32[]{:S(2)}) async-start(bf16[32,24,1024]{2,1,0:T(8,128)(2,1)} %bitcast.37), calls=%async_computation.3 | async-start | bytes 3145728 | tf_op jit(solution)/shard_map/all_to_all | solution.py:259
  156.8 0.8 copy.99
  157.6 0.3 iota_compare_fusion
  157.9 0.1 add_convert_fusion.sel_ref
  158.0 21.5 %all-to-all-done.3 = bf16[32,24,1024]{2,1,0:T(8,128)(2,1)S(1)} async-done(((bf16[32,24,1024]{2,1,0:T(8,128)(2,1)}), bf16[32,24,1024]{2,1,0:T(8,128)(2,1)S(1)}, u32[]{:S(2)}, u32[]{:S(2)}) %all-to-all-start.3) | async-done | bytes 1572896 | tf_op jit(solution)/shard_map/all_to_all | solution.py:259
  179.5 0.9 copy-done.1
  180.4 2.1 %shard_map.138 = f32[256,1024]{1,0:T(8,128)} custom-call(bf16[768,1024]{1,0:T(8,128)(2,1)S(1)} %bitcast.165, f32[256,1024]{1,0:T(8,128)S(1)} %get-tuple-element.8.hres_ref, bf16[2,256,768]{2,1,0:T(8,128)(2,1)S(1)} %add_convert_fusion.sel_ref, f32[256,2]{1,0:T(8,128)S(1)} %bitcast.167), custom_call_target="tpu_custom_call" | custom-call | tf_op jit(solution)/shard_map/pallas_call | solution.py:171
  (41 shorter events, 0.4 us)
Async XLA Ops:
  6.5 44.4 %copy-start = (f32[1,256,128]{2,1,0:T(8,128)S(1)}, f32[1,256,128]{2,1,0:T(8,128)}, u32[]{:S(2)}) copy-start(f32[1,256,128]{2,1,0:T(8,128)} %param.17) | copy-start | bytes 393220
  6.5 6.0 %copy-start.4 = (f32[1,256,128]{2,1,0:T(8,128)S(1)}, f32[1,256,128]{2,1,0:T(8,128)}, u32[]{:S(2)}) copy-start(f32[1,256,128]{2,1,0:T(8,128)} %param.16) | copy-start | bytes 393220
  6.5 128.3 %all-gather.3.cloned.1.call-start = ((), (), s32[]{:S(2)}) async-start(), calls=%async_computation.4 | async-start | bytes 10027008 | tf_op jit(solution)/shard_map/all_gather | solution.py:208
  6.5 14.3 %copy-start.5 = (s32[1,256,2]{1,2,0:T(2,128)S(1)}, s32[1,256,2]{1,2,0:T(2,128)}, u32[]{:S(2)}) copy-start(s32[1,256,2]{1,2,0:T(2,128)} %param.26) | copy-start | bytes 6148
  10.7 30.0 %copy-start.2 = (bf16[1,256,1024]{2,1,0:T(8,128)(2,1)S(1)}, bf16[1,256,1024]{2,1,0:T(8,128)(2,1)}, u32[]{:S(2)}) copy-start(bf16[1,256,1024]{2,1,0:T(8,128)(2,1)} %param.15) | copy-start | bytes 1572868
  13.5 37.8 %copy-start.9 = (f32[16]{0:T(128)S(1)}, f32[16]{0:T(128)}, u32[]{:S(2)}) copy-start(f32[16]{0:T(128)} %param.19) | copy-start | bytes 196
  14.4 12.3 %all-to-all-start = ((f16[16,72,128]{2,1,0:T(8,128)(2,1)}), f16[16,72,128]{2,1,0:T(8,128)(2,1)S(1)}, u32[]{:S(2)}, u32[]{:S(2)}) async-start(f16[16,72,128]{2,1,0:T(8,128)(2,1)} %pad_maximum_fusion), calls=%async_computation | async-start | bytes 589824 | tf_op jit(solution)/shard_map/all_to_all | solution.py:53
  26.9 13.1 %collective-permute-start = (f16[4,64,128]{2,1,0:T(8,128)(2,1)S(1)}, f16[4,64,128]{2,1,0:T(8,128)(2,1)S(1)}, u32[]{:S(2)}, u32[]{:S(2)}) collective-permute-start(f16[4,64,128]{2,1,0:T(8,128)(2,1)S(1)} %get-tuple-element.11), channel_id=1, source_target_pairs={{0,128},{32,160},{64,192},{96,224},{1,129},{33,161},{65,193},{97,2... | collective-permute-start | bytes 196616 | tf_op jit(solution)/shard_map/ppermute | solution.py:66
  40.1 1.9 collective-permute-start.1
  42.0 0.7 collective-permute-start.2
  43.6 17.6 %all-to-all-start.1 = ((f16[16,64,128]{2,1,0:T(8,128)(2,1)}), f16[16,64,128]{2,1,0:T(8,128)(2,1)S(1)}, u32[]{:S(2)}, u32[]{:S(2)}) async-start(f16[16,64,128]{2,1,0:T(8,128)(2,1)} %pad_maximum_fusion.1), calls=%async_computation.1 | async-start | bytes 524288 | tf_op jit(solution)/shard_map/all_to_all | solution.py:72
  51.4 9.9 %copy-start.3 = (f32[1,256,1024]{1,2,0:T(8,128)S(1)}, f32[1,256,1024]{1,2,0:T(8,128)}, u32[]{:S(2)}) copy-start(f32[1,256,1024]{1,2,0:T(8,128)} %copy.98) | copy-start | bytes 3145732
  57.5 8.6 %copy-start.6 = (f32[1024]{0:T(1024)S(1)}, f32[1024]{0:T(1024)}, u32[]{:S(2)}) copy-start(f32[1024]{0:T(1024)} %param.21) | copy-start | bytes 12292
  64.5 3.4 %copy-start.8 = (f32[1024]{0:T(1024)S(1)}, f32[1024]{0:T(1024)}, u32[]{:S(2)}) copy-start(f32[1024]{0:T(1024)} %param.22) | copy-start | bytes 12292
  134.8 21.9 %copy-start.7 = (f32[1,256,2]{1,2,0:T(2,128)S(1)}, f32[1,256,2]{1,2,0:T(2,128)}, u32[]{:S(2)}) copy-start(f32[1,256,2]{1,2,0:T(2,128)} %param.27) | copy-start | bytes 6148
  147.6 31.8 %all-to-all-start.3 = ((bf16[32,24,1024]{2,1,0:T(8,128)(2,1)}), bf16[32,24,1024]{2,1,0:T(8,128)(2,1)S(1)}, u32[]{:S(2)}, u32[]{:S(2)}) async-start(bf16[32,24,1024]{2,1,0:T(8,128)(2,1)} %bitcast.37), calls=%async_computation.3 | async-start | bytes 3145728 | tf_op jit(solution)/shard_map/all_to_all | solution.py:259
  179.5 0.9 copy-start.1
Sparse Core Ops, SparseCore 0:
  9.4 125.3 all-gather.2

commit v4 on v3

--- a/solution.py
+++ b/solution.py
@@ -86,28 +86,26 @@
     out_rows = total // 3
 
     def body(x_ref, w_ref, out_ref, w_buf, hid_ref, out_buf, w_sems, out_sems):
-        def copy(block, part):
+        def copy(block):
             first, count = blocks[block]
             return pltpu.make_async_copy(
-                w_ref.at[part, first : first + count, :],
-                w_buf.at[part, first : first + count, :],
-                w_sems.at[block, part],
+                w_ref.at[:, first : first + count, :],
+                w_buf.at[:, first : first + count, :],
+                w_sems.at[block],
             )
 
         for block in order:
-            for part in range(parts):
-                copy(block, part).start()
+            copy(block).start()
 
         def matrix(block):
             first, count = blocks[block]
-            for part in range(parts):
-                copy(block, part).wait()
+            copy(block).wait()
             return w_buf[:, first : first + count, :].reshape(parts * count, FF_BLOCK)
 
         for f in range(ff_steps):
-            x = x_ref[...]
-            gate = jnp.dot(x, matrix(f), preferred_element_type=f32)
-            upper = jnp.dot(x, matrix(ff_steps + f), preferred_element_type=f32)
+            w_gate, w_up = matrix(f), matrix(ff_steps + f)
+            gate = jnp.dot(x_ref[...], w_gate, preferred_element_type=f32)
+            upper = jnp.dot(x_ref[...], w_up, preferred_element_type=f32)
             hidden = (gate / (1.0 + jnp.exp(-gate))) * upper
             hid_ref[:, f * FF_BLOCK : (f + 1) * FF_BLOCK] = hidden.astype(bf16)
         sides = [matrix(block) for block in down]
@@ -136,31 +134,26 @@
             pltpu.VMEM((parts, packed, FF_BLOCK), bf16),
             pltpu.VMEM((total, hidden_width), bf16),
             pltpu.VMEM((total, model_width), bf16),
-            pltpu.SemaphoreType.DMA((len(blocks), parts)),
+            pltpu.SemaphoreType.DMA((len(blocks),)),
             pltpu.SemaphoreType.DMA((3,)),
         ],
         compiler_params=pltpu.CompilerParams(vmem_limit_bytes=32 * MIB),
     )(rows, pltpu.with_memory_space_constraint(weights, pltpu.HBM))
 
 
-def combine(back, hres, selection, route_weights):
+def combine(back, hres, selection):
     length, model_width = hres.shape
     block = 256
     steps = model_width // block
 
-    def body(back_ref, hres_ref, sel_ref, weight_in, out_ref, out_buf, weight_ref, sems):
-        arriving = pltpu.make_async_copy(weight_in, weight_ref, sems.at[steps])
-        arriving.start()
+    def body(back_ref, hres_ref, sel_ref, out_ref, out_buf, sems):
         leaving = []
         for i in range(steps):
             part = slice(i * block, (i + 1) * block)
             rows = back_ref[:, part]
             first = jnp.dot(sel_ref[0], rows, preferred_element_type=f32)
             second = jnp.dot(sel_ref[1], rows, preferred_element_type=f32)
-            if i == 0:
-                arriving.wait()
-                weight_a, weight_b = weight_ref[:, 0:1], weight_ref[:, 1:2]
-            out_buf[:, part] = hres_ref[:, part] + (weight_a * first + weight_b * second)
+            out_buf[:, part] = hres_ref[:, part] + (first + second)
             leaving.append(
                 pltpu.make_async_copy(out_buf.at[:, part], out_ref.at[:, part], sems.at[i])
             )
@@ -170,16 +163,12 @@
 
     return pl.pallas_call(
         body,
-        in_specs=[pl.BlockSpec(memory_space=pltpu.VMEM)] * 3 + [pl.BlockSpec(memory_space=pl.ANY)],
+        in_specs=[pl.BlockSpec(memory_space=pltpu.VMEM)] * 3,
         out_specs=pl.BlockSpec(memory_space=pl.ANY),
         out_shape=jax.ShapeDtypeStruct((length, model_width), f32),
-        scratch_shapes=[
-            pltpu.VMEM((length, model_width), f32),
-            pltpu.VMEM(route_weights.shape, f32),
-            pltpu.SemaphoreType.DMA((steps + 1,)),
-        ],
+        scratch_shapes=[pltpu.VMEM((length, model_width), f32), pltpu.SemaphoreType.DMA((steps,))],
         compiler_params=pltpu.CompilerParams(vmem_limit_bytes=16 * MIB),
-    )(back, hres, selection, route_weights)
+    )(back, hres, selection)
 
 
 def per_device(
@@ -246,8 +235,16 @@
     spread = (
         (targets[:, 0][None, :] == slot_ids[:, None]) | (targets[:, 1][None, :] == slot_ids[:, None])
     ).astype(bf16)
+    weights = route_weights[0]
+    leading = lax.reduce_precision(weights, 8, 7)
     selection = jnp.stack(
-        [targets[:, k : k + 1] == slot_ids[None, :] for k in range(targets.shape[1])]
+        [
+            sum(
+                jnp.where(targets[:, k : k + 1] == slot_ids[None, :], half[:, k : k + 1], 0.0)
+                for k in range(targets.shape[1])
+            )
+            for half in (leading, weights - leading)
+        ]
     ).astype(bf16)
     outgoing = jnp.dot(spread, normed, preferred_element_type=f32).astype(bf16)
     received = lax.all_to_all(
@@ -259,7 +256,7 @@
     back = lax.all_to_all(
         produced.reshape(experts, capacity, model_width), "expert", 0, 0, tiled=True
     )
-    out = combine(back.reshape(experts * capacity, model_width), hres, selection, route_weights[0])
+    out = combine(back.reshape(experts * capacity, model_width), hres, selection)
     return out.reshape(1, length, model_width)
 
 

time: 190 us -> 187 us (0.984)
  Pallas kernels: 16.8 us -> 14.5 us
    pallas_call x1, Pallas kernels: 12.8 us -> 10.6 us  [expert_layer(): pl.pallas_call(body, in_specs=[pl.BlockSpec(memory_space=pltpu.VMEM), any...]
where the time goes in v4:
time: 187 us; the launch traced here: 186 us
  waiting for transfers between devices  67.6 us (36%)
  starting transfers between devices  35.4 us (19%)
  blocking collectives  32.2 us (17%)
  Pallas kernels  14.5 us (8%)
  between operations  13.7 us (7%)
  matrix products  11.7 us (6%)
  local copies, waits for them, and re-layouts  5.95 us (3%)
  other arithmetic  4.99 us (3%)
    all_gather x1, waiting for transfers between devices, per_device(): lax.all_gather(pack_weights(w_gate[0], w_up[0], w_down[0]), 'tm', axis=0)  33.9 us
    all_to_all x1, blocking collectives, per_device(): lax.all_to_all(outgoing.reshape(experts, capacity, model_width), 'expert'...  32.2 us
    all_to_all x1, waiting for transfers between devices, per_device(): lax.all_to_all(produced.reshape(experts, capacity, model_width), 'expert'...  22.2 us
    ppermute x3, starting transfers between devices, incoming_states(): handed = lax.ppermute((passed * entry + total).astype(f16), 'tm', hops)  12.3 us
    pallas_call x1, Pallas kernels, expert_layer(): pl.pallas_call(body, in_specs=[pl.BlockSpec(memory_space=pltpu.VMEM), any...  10.6 us
    all_to_all x1, starting transfers between devices, per_device(): lax.all_to_all(produced.reshape(experts, capacity, model_width), 'expert'...  9.27 us
    all_to_all x1, starting transfers between devices, incoming_states(): lax.all_to_all(returned, 'tm', 0, 0, tiled=True, axis_index_groups=groups)  7.35 us
    all_to_all x1, starting transfers between devices, incoming_states(): lax.all_to_all(sent, 'tm', 0, 0, tiled=True, axis_index_groups=groups)  6.44 us
  transfers between devices with their start and end apart: 7, of which 5 were waited for; matrix products, arithmetic and copies ran while one was open for 12% of the time, Pallas kernels for 0%

profile of v4, /device:TPU:1, one launch (start us, length us, event | category | flops | bytes accessed | tf_op | source)
XLA Modules:
  0.0 186.0 jit_solution(1177625887848271656)
XLA Ops:
  6.5 2.0 %shard_map.136 = bf16[576,512]{1,0:T(8,128)(2,1)} custom-call(bf16[64,1536]{1,0:T(8,128)(2,1)} %bitcast.182, bf16[64,1536]{1,0:T(8,128)(2,1)} %bitcast.183, bf16[96,1024]{1,0:T(8,128)(2,1)} %bitcast.184), custom_call_target="tpu_custom_call" | custom-call | tf_op jit(solution)/shard_map/pallas_call | solution.py:35
  8.6 0.0 all-gather.3.cloned.1.call-update
  8.6 0.7 copy_bitcast_fusion.1
  9.3 0.6 reduce-window.6
  9.9 0.2 slice_reduce_fusion
  10.1 0.1 fusion.49
  10.2 0.2 slice_reduce_fusion.1
  10.4 0.1 copy.86
  10.5 0.1 copy.87
  10.6 0.1 copy.88
  10.6 0.1 stack.16
  10.7 0.0 copy-start.1
  10.7 1.6 copy.84
  12.4 0.1 bitcast_exponential_fusion
  12.5 0.1 bitcast_multiply_fusion.1
  12.6 1.0 convolution_convert_fusion.1
  13.5 0.0 copy-start.8
  13.6 0.1 broadcast_in_dim.106
  13.6 0.8 pad_maximum_fusion.1
  14.4 6.4 %all-to-all-start = ((f16[16,72,128]{2,1,0:T(8,128)(2,1)}), f16[16,72,128]{2,1,0:T(8,128)(2,1)S(1)}, u32[]{:S(2)}, u32[]{:S(2)}) async-start(f16[16,72,128]{2,1,0:T(8,128)(2,1)} %pad_maximum_fusion.1), calls=%async_computation | async-start | bytes 589824 | tf_op jit(solution)/shard_map/all_to_all | solution.py:53
  20.9 0.3 convolution_convert_fusion.2
  21.2 5.6 %all-to-all-done = f16[16,72,128]{2,1,0:T(8,128)(2,1)S(1)} async-done(((f16[16,72,128]{2,1,0:T(8,128)(2,1)}), f16[16,72,128]{2,1,0:T(8,128)(2,1)S(1)}, u32[]{:S(2)}, u32[]{:S(2)}) %all-to-all-start) | async-done | bytes 294944 | tf_op jit(solution)/shard_map/all_to_all | solution.py:53
  26.9 0.1 add_convert_fusion.4
  26.9 11.0 %collective-permute-start = (f16[4,64,128]{2,1,0:T(8,128)(2,1)S(1)}, f16[4,64,128]{2,1,0:T(8,128)(2,1)S(1)}, u32[]{:S(2)}, u32[]{:S(2)}) collective-permute-start(f16[4,64,128]{2,1,0:T(8,128)(2,1)S(1)} %get-tuple-element.11), channel_id=1, source_target_pairs={{0,128},{32,160},{64,192},{96,224},{1,129},{33,161},{65,193},{97,2... | collective-permute-start | bytes 196616 | tf_op jit(solution)/shard_map/ppermute | solution.py:66
  37.9 2.1 %collective-permute-done = f16[4,64,128]{2,1,0:T(8,128)(2,1)S(1)} collective-permute-done((f16[4,64,128]{2,1,0:T(8,128)(2,1)S(1)}, f16[4,64,128]{2,1,0:T(8,128)(2,1)S(1)}, u32[]{:S(2)}, u32[]{:S(2)}) %collective-permute-start) | collective-permute-done | bytes 65568 | tf_op jit(solution)/shard_map/ppermute | solution.py:66
  40.1 0.7 collective-permute-start.1
  40.8 1.2 copy.93
  42.0 0.0 collective-permute-done.1
  42.0 0.7 collective-permute-start.2
  42.7 0.1 fusion.51
  42.8 0.8 pad_maximum_fusion.2
  43.6 7.3 %all-to-all-start.1 = ((f16[16,64,128]{2,1,0:T(8,128)(2,1)}), f16[16,64,128]{2,1,0:T(8,128)(2,1)S(1)}, u32[]{:S(2)}, u32[]{:S(2)}) async-start(f16[16,64,128]{2,1,0:T(8,128)(2,1)} %pad_maximum_fusion.2), calls=%async_computation.1 | async-start | bytes 524288 | tf_op jit(solution)/shard_map/all_to_all | solution.py:72
  51.0 0.4 fusion.37
  51.4 0.0 copy-start.2
  51.4 6.1 %fusion.16 = f32[256,16,64]{0,2,1:T(8,128)} fusion(f32[256,16,64]{0,2,1:T(8,128)S(1)} %bitcast.176, f32[256,256]{1,0:T(8,128)S(1)} %fusion.37, f32[16,256]{1,0:T(8,128)S(1)} %get-tuple-element.24, pred[256,256]{1,0:T(8,128)(4,1)S(1)} %iota_compare_fusion.5, f32[16]{0:T(128)S(1)} %copy-done.8), kind=kOutput, calls=%fused_computation.16 | convolution fusion | flops 810024960 | bytes 2441280 | tf_op jit(solution)/shard_map/hij,jhp->ihp/dot_general | solution.py:214
  57.5 3.7 %all-to-all-done.1 = f16[16,64,128]{2,1,0:T(8,128)(2,1)S(1)} async-done(((f16[16,64,128]{2,1,0:T(8,128)(2,1)}), f16[16,64,128]{2,1,0:T(8,128)(2,1)S(1)}, u32[]{:S(2)}, u32[]{:S(2)}) %all-to-all-start.1) | async-done | bytes 262176 | tf_op jit(solution)/shard_map/all_to_all | solution.py:72
  61.3 3.2 %multiply_reduce_fusion.1 = (f32[256]{0:T(256)S(1)}, f32[256,16,64]{0,2,1:T(8,128)}) fusion(f32[256,16,64]{0,2,1:T(8,128)S(1)} %bitcast.180, f32[256,16,64]{0,2,1:T(8,128)} %fusion.16, f16[16,64,128]{2,1,0:T(8,128)(2,1)S(1)} %all-to-all-done.1, f32[1,256,128]{2,1,0:T(8,128)S(1)} %copy-done, f32[256,16]{0,1:T(8,128)S(1)} %get-tuple-element.21), kind=kOutput, calls=%fused_computation.31 | convolution fusion | flops 405012224 | bytes 3556352 | tf_op jit(solution)/shard_map/in,hpn->ihp/dot_general | solution.py:217
  64.5 1.6 copy.92
  66.1 1.8 multiply_reduce_fusion
  67.9 0.7 convolution_convert_fusion
  68.6 32.2 %all_to_all.20 = bf16[32,24,1024]{2,1,0:T(8,128)(2,1)S(1)} all-to-all(bf16[32,24,1024]{2,1,0:T(8,128)(2,1)S(1)} %bitcast.178), channel_id=1, replica_groups=mesh['tm'=16,'expert'=32] {'expert'}, dimensions={0} | all-to-all | bytes 3145728 | tf_op jit(solution)/shard_map/all_to_all | solution.py:250
  100.8 33.9 %all-gather.3.cloned.1.call-done = bf16[9216,512]{1,0:T(8,128)(2,1)} async-done(((bf16[576,512]{1,0:T(8,128)(2,1)}), bf16[9216,512]{1,0:T(8,128)(2,1)}) %all-gather.3.cloned.1.call-update) | async-done | bytes 9437200 | tf_op jit(solution)/shard_map/all_gather | solution.py:197
  134.7 10.6 %shard_map.137 = bf16[768,1024]{1,0:T(8,128)(2,1)} custom-call(bf16[768,1024]{1,0:T(8,128)(2,1)S(1)} %bitcast.174, bf16[16,576,512]{2,1,0:T(8,128)(2,1)} %bitcast.175), custom_call_target="tpu_custom_call" | custom-call | tf_op jit(solution)/shard_map/pallas_call | solution.py:128
  145.4 9.3 %all-to-all-start.3 = ((bf16[32,24,1024]{2,1,0:T(8,128)(2,1)}), bf16[32,24,1024]{2,1,0:T(8,128)(2,1)S(1)}, u32[]{:S(2)}, u32[]{:S(2)}) async-start(bf16[32,24,1024]{2,1,0:T(8,128)(2,1)} %bitcast.37), calls=%async_computation.3 | async-start | bytes 3145728 | tf_op jit(solution)/shard_map/all_to_all | solution.py:256
  154.7 0.3 add_convert_fusion.1
  155.0 0.1 pad_maximum_fusion.sel_ref
  155.1 22.2 %all-to-all-done.3 = bf16[32,24,1024]{2,1,0:T(8,128)(2,1)S(1)} async-done(((bf16[32,24,1024]{2,1,0:T(8,128)(2,1)}), bf16[32,24,1024]{2,1,0:T(8,128)(2,1)S(1)}, u32[]{:S(2)}, u32[]{:S(2)}) %all-to-all-start.3) | async-done | bytes 1572896 | tf_op jit(solution)/shard_map/all_to_all | solution.py:256
  177.4 1.8 shard_map.138
  (40 shorter events, 0.4 us)
Async XLA Ops:
  6.5 44.5 %copy-start = (f32[1,256,128]{2,1,0:T(8,128)S(1)}, f32[1,256,128]{2,1,0:T(8,128)}, u32[]{:S(2)}) copy-start(f32[1,256,128]{2,1,0:T(8,128)} %param.17) | copy-start | bytes 393220
  6.5 6.0 %copy-start.3 = (f32[1,256,128]{2,1,0:T(8,128)S(1)}, f32[1,256,128]{2,1,0:T(8,128)}, u32[]{:S(2)}) copy-start(f32[1,256,128]{2,1,0:T(8,128)} %param.16) | copy-start | bytes 393220
  6.5 128.2 %all-gather.3.cloned.1.call-start = ((), (), s32[]{:S(2)}) async-start(), calls=%async_computation.4 | async-start | bytes 10027008 | tf_op jit(solution)/shard_map/all_gather | solution.py:197
  6.5 14.3 %copy-start.4 = (s32[1,256,2]{1,2,0:T(2,128)S(1)}, s32[1,256,2]{1,2,0:T(2,128)}, u32[]{:S(2)}) copy-start(s32[1,256,2]{1,2,0:T(2,128)} %param.26) | copy-start | bytes 6148
  10.7 30.0 %copy-start.1 = (bf16[1,256,1024]{2,1,0:T(8,128)(2,1)S(1)}, bf16[1,256,1024]{2,1,0:T(8,128)(2,1)}, u32[]{:S(2)}) copy-start(bf16[1,256,1024]{2,1,0:T(8,128)(2,1)} %param.15) | copy-start | bytes 1572868
  13.5 37.8 %copy-start.8 = (f32[16]{0:T(128)S(1)}, f32[16]{0:T(128)}, u32[]{:S(2)}) copy-start(f32[16]{0:T(128)} %param.19) | copy-start | bytes 196
  14.4 12.3 %all-to-all-start = ((f16[16,72,128]{2,1,0:T(8,128)(2,1)}), f16[16,72,128]{2,1,0:T(8,128)(2,1)S(1)}, u32[]{:S(2)}, u32[]{:S(2)}) async-start(f16[16,72,128]{2,1,0:T(8,128)(2,1)} %pad_maximum_fusion.1), calls=%async_computation | async-start | bytes 589824 | tf_op jit(solution)/shard_map/all_to_all | solution.py:53
  26.9 13.1 %collective-permute-start = (f16[4,64,128]{2,1,0:T(8,128)(2,1)S(1)}, f16[4,64,128]{2,1,0:T(8,128)(2,1)S(1)}, u32[]{:S(2)}, u32[]{:S(2)}) collective-permute-start(f16[4,64,128]{2,1,0:T(8,128)(2,1)S(1)} %get-tuple-element.11), channel_id=1, source_target_pairs={{0,128},{32,160},{64,192},{96,224},{1,129},{33,161},{65,193},{97,2... | collective-permute-start | bytes 196616 | tf_op jit(solution)/shard_map/ppermute | solution.py:66
  40.1 1.9 %collective-permute-start.1 = (f16[4,64,128]{2,1,0:T(8,128)(2,1)S(1)}, f16[4,64,128]{2,1,0:T(8,128)(2,1)S(1)}, u32[]{:S(2)}, u32[]{:S(2)}) collective-permute-start(f16[4,64,128]{2,1,0:T(8,128)(2,1)S(1)} %fusion.33), channel_id=1, source_target_pairs={{128,256},{160,288},{192,320},{224,352},{129,257},{161,289},{193,3... | collective-permute-start | bytes 196616 | tf_op jit(solution)/shard_map/ppermute | solution.py:66
  42.0 0.7 collective-permute-start.2
  43.6 17.6 %all-to-all-start.1 = ((f16[16,64,128]{2,1,0:T(8,128)(2,1)}), f16[16,64,128]{2,1,0:T(8,128)(2,1)S(1)}, u32[]{:S(2)}, u32[]{:S(2)}) async-start(f16[16,64,128]{2,1,0:T(8,128)(2,1)} %pad_maximum_fusion.2), calls=%async_computation.1 | async-start | bytes 524288 | tf_op jit(solution)/shard_map/all_to_all | solution.py:72
  51.4 9.9 %copy-start.2 = (f32[1,256,1024]{1,2,0:T(8,128)S(1)}, f32[1,256,1024]{1,2,0:T(8,128)}, u32[]{:S(2)}) copy-start(f32[1,256,1024]{1,2,0:T(8,128)} %copy.93) | copy-start | bytes 3145732
  57.5 8.6 %copy-start.5 = (f32[1024]{0:T(1024)S(1)}, f32[1024]{0:T(1024)}, u32[]{:S(2)}) copy-start(f32[1024]{0:T(1024)} %param.21) | copy-start | bytes 12292
  64.5 3.4 %copy-start.7 = (f32[1024]{0:T(1024)S(1)}, f32[1024]{0:T(1024)}, u32[]{:S(2)}) copy-start(f32[1024]{0:T(1024)} %param.22) | copy-start | bytes 12292
  134.7 19.9 %copy-start.6 = (f32[1,256,2]{1,2,0:T(2,128)S(1)}, f32[1,256,2]{1,2,0:T(2,128)}, u32[]{:S(2)}) copy-start(f32[1,256,2]{1,2,0:T(2,128)} %param.27) | copy-start | bytes 6148
  145.4 32.0 %all-to-all-start.3 = ((bf16[32,24,1024]{2,1,0:T(8,128)(2,1)}), bf16[32,24,1024]{2,1,0:T(8,128)(2,1)S(1)}, u32[]{:S(2)}, u32[]{:S(2)}) async-start(bf16[32,24,1024]{2,1,0:T(8,128)(2,1)} %bitcast.37), calls=%async_computation.3 | async-start | bytes 3145728 | tf_op jit(solution)/shard_map/all_to_all | solution.py:256
Sparse Core Ops, SparseCore 0:
  9.4 125.2 all-gather.2

commit v5 on v4

--- a/solution.py
+++ b/solution.py
@@ -79,63 +79,50 @@
     f_rows = hidden_width // parts
     ff_steps = hidden_width // FF_BLOCK
     out_steps = model_width // FF_BLOCK
-    blocks = [(k_rows * i, k_rows) for i in range(2 * ff_steps)]
-    blocks += [(2 * ff_steps * k_rows + f_rows * i, f_rows) for i in range(out_steps)]
-    down = list(range(2 * ff_steps, len(blocks)))
-    order = [b for f in range(ff_steps) for b in (f, ff_steps + f)] + down
-    out_rows = total // 3
-
-    def body(x_ref, w_ref, out_ref, w_buf, hid_ref, out_buf, w_sems, out_sems):
+    gates = [(k_rows * i, k_rows, 0, FF_BLOCK) for i in range(2 * ff_steps)]
+    downs = [(2 * ff_steps * k_rows + f_rows * i, f_rows, 0, FF_BLOCK) for i in range(out_steps)]
+    half = FF_BLOCK // 2
+    pairs = [
+        ((0, k_rows, at, half), (ff_steps * k_rows, k_rows, at, half), at) for at in (0, half)
+    ]
+    pairs += [(gates[f], gates[ff_steps + f], f * FF_BLOCK) for f in range(1, ff_steps)]
+    order = [block for pair in pairs for block in pair[:2]] + downs
+
+    def body(x_ref, w_ref, out_ref, w_buf, hid_ref, sems):
         def copy(block):
-            first, count = blocks[block]
-            return pltpu.make_async_copy(
-                w_ref.at[:, first : first + count, :],
-                w_buf.at[:, first : first + count, :],
-                w_sems.at[block],
-            )
+            first, rows, at, columns = block
+            place = (slice(None), slice(first, first + rows), slice(at, at + columns))
+            return pltpu.make_async_copy(w_ref.at[place], w_buf.at[place], sems.at[order.index(block)])
 
         for block in order:
             copy(block).start()
 
         def matrix(block):
-            first, count = blocks[block]
+            first, rows, at, columns = block
             copy(block).wait()
-            return w_buf[:, first : first + count, :].reshape(parts * count, FF_BLOCK)
-
-        for f in range(ff_steps):
-            w_gate, w_up = matrix(f), matrix(ff_steps + f)
+            return w_buf[:, first : first + rows, at : at + columns].reshape(parts * rows, columns)
+
+        for gate_block, up_block, at in pairs:
+            w_gate, w_up = matrix(gate_block), matrix(up_block)
             gate = jnp.dot(x_ref[...], w_gate, preferred_element_type=f32)
             upper = jnp.dot(x_ref[...], w_up, preferred_element_type=f32)
             hidden = (gate / (1.0 + jnp.exp(-gate))) * upper
-            hid_ref[:, f * FF_BLOCK : (f + 1) * FF_BLOCK] = hidden.astype(bf16)
-        sides = [matrix(block) for block in down]
-        leaving = []
-        for i, r in enumerate(range(0, total, out_rows)):
-            for n, side in enumerate(sides):
-                out_buf[r : r + out_rows, n * FF_BLOCK : (n + 1) * FF_BLOCK] = jnp.dot(
-                    hid_ref[r : r + out_rows, :], side, preferred_element_type=f32
-                ).astype(bf16)
-            leaving.append(
-                pltpu.make_async_copy(
-                    out_buf.at[r : r + out_rows, :], out_ref.at[r : r + out_rows, :], out_sems.at[i]
-                )
-            )
-            leaving[-1].start()
-        for each in leaving:
-            each.wait()
-
-    anywhere = pl.BlockSpec(memory_space=pl.ANY)
+            hid_ref[:, at : at + gate_block[3]] = hidden.astype(bf16)
+        for n, block in enumerate(downs):
+            out_ref[:, n * FF_BLOCK : (n + 1) * FF_BLOCK] = jnp.dot(
+                hid_ref[...], matrix(block), preferred_element_type=f32
+            ).astype(bf16)
+
+    in_vmem = pl.BlockSpec(memory_space=pltpu.VMEM)
     return pl.pallas_call(
         body,
-        in_specs=[pl.BlockSpec(memory_space=pltpu.VMEM), anywhere],
-        out_specs=anywhere,
-        out_shape=jax.ShapeDtypeStruct((total, model_width), bf16),
+        in_specs=[in_vmem, pl.BlockSpec(memory_space=pl.ANY)],
+        out_specs=in_vmem,
+        out_shape=pltpu.VMEM((total, model_width), bf16),
         scratch_shapes=[
             pltpu.VMEM((parts, packed, FF_BLOCK), bf16),
             pltpu.VMEM((total, hidden_width), bf16),
-            pltpu.VMEM((total, model_width), bf16),
-            pltpu.SemaphoreType.DMA((len(blocks),)),
-            pltpu.SemaphoreType.DMA((3,)),
+            pltpu.SemaphoreType.DMA((len(order),)),
         ],
         compiler_params=pltpu.CompilerParams(vmem_limit_bytes=32 * MIB),
     )(rows, pltpu.with_memory_space_constraint(weights, pltpu.HBM))

time: 187 us -> 187 us (level)
  no operation moved by 1% of the time
where the time goes in v5:
time: 187 us; the launch traced here: 186 us
  waiting for transfers between devices  67.6 us (36%)
  starting transfers between devices  35.4 us (19%)
  blocking collectives  32.2 us (17%)
  Pallas kernels  14.8 us (8%)
  between operations  13.7 us (7%)
  matrix products  11.7 us (6%)
  local copies, waits for them, and re-layouts  5.95 us (3%)
  other arithmetic  4.99 us (3%)
    all_gather x1, waiting for transfers between devices, per_device(): lax.all_gather(pack_weights(w_gate[0], w_up[0], w_down[0]), 'tm', axis=0)  33.9 us
    all_to_all x1, blocking collectives, per_device(): lax.all_to_all(outgoing.reshape(experts, capacity, model_width), 'expert'...  32.2 us
    all_to_all x1, waiting for transfers between devices, per_device(): lax.all_to_all(produced.reshape(experts, capacity, model_width), 'expert'...  22.2 us
    ppermute x3, starting transfers between devices, incoming_states(): handed = lax.ppermute((passed * entry + total).astype(f16), 'tm', hops)  12.3 us
    pallas_call x1, Pallas kernels, expert_layer(): pl.pallas_call(body, in_specs=[in_vmem, pl.BlockSpec(memory_space=pl.ANY)...  11 us
    all_to_all x1, starting transfers between devices, per_device(): lax.all_to_all(produced.reshape(experts, capacity, model_width), 'expert'...  9.27 us
    all_to_all x1, starting transfers between devices, incoming_states(): lax.all_to_all(returned, 'tm', 0, 0, tiled=True, axis_index_groups=groups)  7.35 us
    all_to_all x1, starting transfers between devices, incoming_states(): lax.all_to_all(sent, 'tm', 0, 0, tiled=True, axis_index_groups=groups)  6.44 us
  transfers between devices with their start and end apart: 7, of which 5 were waited for; matrix products, arithmetic and copies ran while one was open for 12% of the time, Pallas kernels for 0%

profile of v5, /device:TPU:1, one launch (start us, length us, event | category | flops | bytes accessed | tf_op | source)
XLA Modules:
  0.0 186.4 jit_solution(17144693747483709822)
XLA Ops:
  6.5 2.0 %shard_map.136 = bf16[576,512]{1,0:T(8,128)(2,1)} custom-call(bf16[64,1536]{1,0:T(8,128)(2,1)} %bitcast.182, bf16[64,1536]{1,0:T(8,128)(2,1)} %bitcast.183, bf16[96,1024]{1,0:T(8,128)(2,1)} %bitcast.184), custom_call_target="tpu_custom_call" | custom-call | tf_op jit(solution)/shard_map/pallas_call | solution.py:35
  8.6 0.0 all-gather.3.cloned.1.call-update
  8.6 0.7 copy_bitcast_fusion.1
  9.3 0.6 reduce-window.6
  9.9 0.2 slice_reduce_fusion
  10.1 0.1 fusion.49
  10.2 0.2 slice_reduce_fusion.1
  10.4 0.1 copy.86
  10.5 0.1 copy.87
  10.6 0.1 copy.88
  10.6 0.1 stack.16
  10.7 0.0 copy-start.1
  10.7 1.6 copy.84
  12.4 0.1 bitcast_exponential_fusion
  12.5 0.1 bitcast_multiply_fusion.1
  12.6 1.0 convolution_convert_fusion.1
  13.5 0.0 copy-start.8
  13.6 0.1 broadcast_in_dim.106
  13.6 0.8 pad_maximum_fusion.1
  14.4 6.4 %all-to-all-start = ((f16[16,72,128]{2,1,0:T(8,128)(2,1)}), f16[16,72,128]{2,1,0:T(8,128)(2,1)S(1)}, u32[]{:S(2)}, u32[]{:S(2)}) async-start(f16[16,72,128]{2,1,0:T(8,128)(2,1)} %pad_maximum_fusion.1), calls=%async_computation | async-start | bytes 589824 | tf_op jit(solution)/shard_map/all_to_all | solution.py:53
  20.9 0.3 convolution_convert_fusion.2
  21.2 5.6 %all-to-all-done = f16[16,72,128]{2,1,0:T(8,128)(2,1)S(1)} async-done(((f16[16,72,128]{2,1,0:T(8,128)(2,1)}), f16[16,72,128]{2,1,0:T(8,128)(2,1)S(1)}, u32[]{:S(2)}, u32[]{:S(2)}) %all-to-all-start) | async-done | bytes 294944 | tf_op jit(solution)/shard_map/all_to_all | solution.py:53
  26.9 0.1 add_convert_fusion.4
  26.9 11.0 %collective-permute-start = (f16[4,64,128]{2,1,0:T(8,128)(2,1)S(1)}, f16[4,64,128]{2,1,0:T(8,128)(2,1)S(1)}, u32[]{:S(2)}, u32[]{:S(2)}) collective-permute-start(f16[4,64,128]{2,1,0:T(8,128)(2,1)S(1)} %get-tuple-element.11), channel_id=1, source_target_pairs={{0,128},{32,160},{64,192},{96,224},{1,129},{33,161},{65,193},{97,2... | collective-permute-start | bytes 196616 | tf_op jit(solution)/shard_map/ppermute | solution.py:66
  37.9 2.1 %collective-permute-done = f16[4,64,128]{2,1,0:T(8,128)(2,1)S(1)} collective-permute-done((f16[4,64,128]{2,1,0:T(8,128)(2,1)S(1)}, f16[4,64,128]{2,1,0:T(8,128)(2,1)S(1)}, u32[]{:S(2)}, u32[]{:S(2)}) %collective-permute-start) | collective-permute-done | bytes 65568 | tf_op jit(solution)/shard_map/ppermute | solution.py:66
  40.1 0.7 collective-permute-start.1
  40.8 1.2 copy.93
  42.0 0.0 collective-permute-done.1
  42.0 0.7 collective-permute-start.2
  42.7 0.1 fusion.51
  42.8 0.8 pad_maximum_fusion.2
  43.6 7.3 %all-to-all-start.1 = ((f16[16,64,128]{2,1,0:T(8,128)(2,1)}), f16[16,64,128]{2,1,0:T(8,128)(2,1)S(1)}, u32[]{:S(2)}, u32[]{:S(2)}) async-start(f16[16,64,128]{2,1,0:T(8,128)(2,1)} %pad_maximum_fusion.2), calls=%async_computation.1 | async-start | bytes 524288 | tf_op jit(solution)/shard_map/all_to_all | solution.py:72
  51.0 0.4 fusion.37
  51.4 0.0 copy-start.2
  51.4 6.1 %fusion.16 = f32[256,16,64]{0,2,1:T(8,128)} fusion(f32[256,16,64]{0,2,1:T(8,128)S(1)} %bitcast.176, f32[256,256]{1,0:T(8,128)S(1)} %fusion.37, f32[16,256]{1,0:T(8,128)S(1)} %get-tuple-element.24, pred[256,256]{1,0:T(8,128)(4,1)S(1)} %iota_compare_fusion.5, f32[16]{0:T(128)S(1)} %copy-done.8), kind=kOutput, calls=%fused_computation.16 | convolution fusion | flops 810024960 | bytes 2441280 | tf_op jit(solution)/shard_map/hij,jhp->ihp/dot_general | solution.py:201
  57.5 3.7 %all-to-all-done.1 = f16[16,64,128]{2,1,0:T(8,128)(2,1)S(1)} async-done(((f16[16,64,128]{2,1,0:T(8,128)(2,1)}), f16[16,64,128]{2,1,0:T(8,128)(2,1)S(1)}, u32[]{:S(2)}, u32[]{:S(2)}) %all-to-all-start.1) | async-done | bytes 262176 | tf_op jit(solution)/shard_map/all_to_all | solution.py:72
  61.3 3.2 %multiply_reduce_fusion.1 = (f32[256]{0:T(256)S(1)}, f32[256,16,64]{0,2,1:T(8,128)}) fusion(f32[256,16,64]{0,2,1:T(8,128)S(1)} %bitcast.180, f32[256,16,64]{0,2,1:T(8,128)} %fusion.16, f16[16,64,128]{2,1,0:T(8,128)(2,1)S(1)} %all-to-all-done.1, f32[1,256,128]{2,1,0:T(8,128)S(1)} %copy-done, f32[256,16]{0,1:T(8,128)S(1)} %get-tuple-element.21), kind=kOutput, calls=%fused_computation.31 | convolution fusion | flops 405012224 | bytes 3556352 | tf_op jit(solution)/shard_map/in,hpn->ihp/dot_general | solution.py:204
  64.5 1.6 copy.92
  66.1 1.8 multiply_reduce_fusion
  67.9 0.7 convolution_convert_fusion
  68.6 32.2 %all_to_all.20 = bf16[32,24,1024]{2,1,0:T(8,128)(2,1)S(1)} all-to-all(bf16[32,24,1024]{2,1,0:T(8,128)(2,1)S(1)} %bitcast.178), channel_id=1, replica_groups=mesh['tm'=16,'expert'=32] {'expert'}, dimensions={0} | all-to-all | bytes 3145728 | tf_op jit(solution)/shard_map/all_to_all | solution.py:237
  100.8 33.9 %all-gather.3.cloned.1.call-done = bf16[9216,512]{1,0:T(8,128)(2,1)} async-done(((bf16[576,512]{1,0:T(8,128)(2,1)}), bf16[9216,512]{1,0:T(8,128)(2,1)}) %all-gather.3.cloned.1.call-update) | async-done | bytes 9437200 | tf_op jit(solution)/shard_map/all_gather | solution.py:184
  134.7 11.0 %shard_map.137 = bf16[768,1024]{1,0:T(8,128)(2,1)} custom-call(bf16[768,1024]{1,0:T(8,128)(2,1)S(1)} %bitcast.174, bf16[16,576,512]{2,1,0:T(8,128)(2,1)} %bitcast.175), custom_call_target="tpu_custom_call" | custom-call | tf_op jit(solution)/shard_map/pallas_call | solution.py:117
  145.7 9.3 %all-to-all-start.3 = ((bf16[32,24,1024]{2,1,0:T(8,128)(2,1)}), bf16[32,24,1024]{2,1,0:T(8,128)(2,1)S(1)}, u32[]{:S(2)}, u32[]{:S(2)}) async-start(bf16[32,24,1024]{2,1,0:T(8,128)(2,1)} %bitcast.37), calls=%async_computation.3 | async-start | bytes 3145728 | tf_op jit(solution)/shard_map/all_to_all | solution.py:243
  155.0 0.3 add_convert_fusion.1
  155.3 0.1 pad_maximum_fusion.sel_ref
  155.4 22.2 %all-to-all-done.3 = bf16[32,24,1024]{2,1,0:T(8,128)(2,1)S(1)} async-done(((bf16[32,24,1024]{2,1,0:T(8,128)(2,1)}), bf16[32,24,1024]{2,1,0:T(8,128)(2,1)S(1)}, u32[]{:S(2)}, u32[]{:S(2)}) %all-to-all-start.3) | async-done | bytes 1572896 | tf_op jit(solution)/shard_map/all_to_all | solution.py:243
  177.7 1.8 shard_map.138
  (40 shorter events, 0.4 us)
Async XLA Ops:
  6.5 44.5 %copy-start = (f32[1,256,128]{2,1,0:T(8,128)S(1)}, f32[1,256,128]{2,1,0:T(8,128)}, u32[]{:S(2)}) copy-start(f32[1,256,128]{2,1,0:T(8,128)} %param.17) | copy-start | bytes 393220
  6.5 6.0 %copy-start.3 = (f32[1,256,128]{2,1,0:T(8,128)S(1)}, f32[1,256,128]{2,1,0:T(8,128)}, u32[]{:S(2)}) copy-start(f32[1,256,128]{2,1,0:T(8,128)} %param.16) | copy-start | bytes 393220
  6.5 128.2 %all-gather.3.cloned.1.call-start = ((), (), s32[]{:S(2)}) async-start(), calls=%async_computation.4 | async-start | bytes 10027008 | tf_op jit(solution)/shard_map/all_gather | solution.py:184
  6.5 14.3 %copy-start.4 = (s32[1,256,2]{1,2,0:T(2,128)S(1)}, s32[1,256,2]{1,2,0:T(2,128)}, u32[]{:S(2)}) copy-start(s32[1,256,2]{1,2,0:T(2,128)} %param.26) | copy-start | bytes 6148
  10.7 30.0 %copy-start.1 = (bf16[1,256,1024]{2,1,0:T(8,128)(2,1)S(1)}, bf16[1,256,1024]{2,1,0:T(8,128)(2,1)}, u32[]{:S(2)}) copy-start(bf16[1,256,1024]{2,1,0:T(8,128)(2,1)} %param.15) | copy-start | bytes 1572868
  13.5 37.8 %copy-start.8 = (f32[16]{0:T(128)S(1)}, f32[16]{0:T(128)}, u32[]{:S(2)}) copy-start(f32[16]{0:T(128)} %param.19) | copy-start | bytes 196
  14.4 12.3 %all-to-all-start = ((f16[16,72,128]{2,1,0:T(8,128)(2,1)}), f16[16,72,128]{2,1,0:T(8,128)(2,1)S(1)}, u32[]{:S(2)}, u32[]{:S(2)}) async-start(f16[16,72,128]{2,1,0:T(8,128)(2,1)} %pad_maximum_fusion.1), calls=%async_computation | async-start | bytes 589824 | tf_op jit(solution)/shard_map/all_to_all | solution.py:53
  26.9 13.1 %collective-permute-start = (f16[4,64,128]{2,1,0:T(8,128)(2,1)S(1)}, f16[4,64,128]{2,1,0:T(8,128)(2,1)S(1)}, u32[]{:S(2)}, u32[]{:S(2)}) collective-permute-start(f16[4,64,128]{2,1,0:T(8,128)(2,1)S(1)} %get-tuple-element.11), channel_id=1, source_target_pairs={{0,128},{32,160},{64,192},{96,224},{1,129},{33,161},{65,193},{97,2... | collective-permute-start | bytes 196616 | tf_op jit(solution)/shard_map/ppermute | solution.py:66
  40.1 1.9 %collective-permute-start.1 = (f16[4,64,128]{2,1,0:T(8,128)(2,1)S(1)}, f16[4,64,128]{2,1,0:T(8,128)(2,1)S(1)}, u32[]{:S(2)}, u32[]{:S(2)}) collective-permute-start(f16[4,64,128]{2,1,0:T(8,128)(2,1)S(1)} %fusion.33), channel_id=1, source_target_pairs={{128,256},{160,288},{192,320},{224,352},{129,257},{161,289},{193,3... | collective-permute-start | bytes 196616 | tf_op jit(solution)/shard_map/ppermute | solution.py:66
  42.0 0.7 collective-permute-start.2
  43.6 17.6 %all-to-all-start.1 = ((f16[16,64,128]{2,1,0:T(8,128)(2,1)}), f16[16,64,128]{2,1,0:T(8,128)(2,1)S(1)}, u32[]{:S(2)}, u32[]{:S(2)}) async-start(f16[16,64,128]{2,1,0:T(8,128)(2,1)} %pad_maximum_fusion.2), calls=%async_computation.1 | async-start | bytes 524288 | tf_op jit(solution)/shard_map/all_to_all | solution.py:72
  51.4 9.9 %copy-start.2 = (f32[1,256,1024]{1,2,0:T(8,128)S(1)}, f32[1,256,1024]{1,2,0:T(8,128)}, u32[]{:S(2)}) copy-start(f32[1,256,1024]{1,2,0:T(8,128)} %copy.93) | copy-start | bytes 3145732
  57.5 8.6 %copy-start.5 = (f32[1024]{0:T(1024)S(1)}, f32[1024]{0:T(1024)}, u32[]{:S(2)}) copy-start(f32[1024]{0:T(1024)} %param.21) | copy-start | bytes 12292
  64.5 3.4 %copy-start.7 = (f32[1024]{0:T(1024)S(1)}, f32[1024]{0:T(1024)}, u32[]{:S(2)}) copy-start(f32[1024]{0:T(1024)} %param.22) | copy-start | bytes 12292
  134.7 20.3 %copy-start.6 = (f32[1,256,2]{1,2,0:T(2,128)S(1)}, f32[1,256,2]{1,2,0:T(2,128)}, u32[]{:S(2)}) copy-start(f32[1,256,2]{1,2,0:T(2,128)} %param.27) | copy-start | bytes 6148
  145.7 32.0 %all-to-all-start.3 = ((bf16[32,24,1024]{2,1,0:T(8,128)(2,1)}), bf16[32,24,1024]{2,1,0:T(8,128)(2,1)S(1)}, u32[]{:S(2)}, u32[]{:S(2)}) async-start(bf16[32,24,1024]{2,1,0:T(8,128)(2,1)} %bitcast.37), calls=%async_computation.3 | async-start | bytes 3145728 | tf_op jit(solution)/shard_map/all_to_all | solution.py:243
Sparse Core Ops, SparseCore 0:
  9.4 125.2 all-gather.2

commit v6 on v4

--- a/solution.py
+++ b/solution.py
@@ -250,6 +250,7 @@
     received = lax.all_to_all(
         outgoing.reshape(experts, capacity, model_width), "expert", 0, 0, tiled=True
     )
+    received, selection = lax.optimization_barrier((received, selection))
     produced = expert_layer(
         received.reshape(experts * capacity, model_width), gathered, model_width, hidden_width
     )

time: 187 us -> 186 us (level)
  transfers between devices with their start and end apart: 7 -> 7, of which waited for: 5 -> 5; matrix products, arithmetic and copies ran while one was open for 12% -> 13% of each run, Pallas kernels for 0% -> 0%
where the time goes in v6:
time: 186 us
  waiting for transfers between devices  66.4 us (36%)
  starting transfers between devices  35.6 us (19%)
  blocking collectives  31.9 us (17%)
  Pallas kernels  14.2 us (8%)
  between operations  13.7 us (7%)
  matrix products  12.8 us (7%)
  local copies, waits for them, and re-layouts  5.95 us (3%)
  other arithmetic  5.02 us (3%)
    all_gather x1, waiting for transfers between devices, per_device(): lax.all_gather(pack_weights(w_gate[0], w_up[0], w_down[0]), 'tm', axis=0)  32.7 us
    all_to_all x1, blocking collectives, per_device(): lax.all_to_all(produced.reshape(experts, capacity, model_width), 'expert'...  31.9 us
    all_to_all x1, waiting for transfers between devices, per_device(): lax.all_to_all(outgoing.reshape(experts, capacity, model_width), 'expert'...  22.2 us
    ppermute x3, starting transfers between devices, incoming_states(): handed = lax.ppermute((passed * entry + total).astype(f16), 'tm', hops)  12.3 us
    pallas_call x1, Pallas kernels, expert_layer(): pl.pallas_call(body, in_specs=[pl.BlockSpec(memory_space=pltpu.VMEM), any...  10.3 us
    all_to_all x1, starting transfers between devices, per_device(): lax.all_to_all(outgoing.reshape(experts, capacity, model_width), 'expert'...  9.54 us
    all_to_all x1, starting transfers between devices, incoming_states(): lax.all_to_all(returned, 'tm', 0, 0, tiled=True, axis_index_groups=groups)  7.35 us
    all_to_all x1, starting transfers between devices, incoming_states(): lax.all_to_all(sent, 'tm', 0, 0, tiled=True, axis_index_groups=groups)  6.44 us
  transfers between devices with their start and end apart: 7, of which 5 were waited for; matrix products, arithmetic and copies ran while one was open for 13% of the time, Pallas kernels for 0%

profile of v6, /device:TPU:1, one launch (start us, length us, event | category | flops | bytes accessed | tf_op | source)
XLA Modules:
  0.0 185.7 jit_solution(2076607945021969221)
XLA Ops:
  6.5 2.0 %shard_map.136 = bf16[576,512]{1,0:T(8,128)(2,1)} custom-call(bf16[64,1536]{1,0:T(8,128)(2,1)} %bitcast.183, bf16[64,1536]{1,0:T(8,128)(2,1)} %bitcast.184, bf16[96,1024]{1,0:T(8,128)(2,1)} %bitcast.185), custom_call_target="tpu_custom_call" | custom-call | tf_op jit(solution)/shard_map/pallas_call | solution.py:35
  8.6 0.0 all-gather.3.cloned.1.call-update
  8.6 0.7 copy_bitcast_fusion.1
  9.3 0.6 reduce-window.6
  9.9 0.2 slice_reduce_fusion
  10.1 0.1 fusion.49
  10.2 0.2 slice_reduce_fusion.1
  10.4 0.1 copy.86
  10.5 0.1 copy.87
  10.6 0.1 copy.88
  10.6 0.1 stack.16
  10.7 0.0 copy-start.1
  10.7 1.6 copy.84
  12.4 0.1 bitcast_exponential_fusion
  12.4 0.1 bitcast_multiply_fusion.1
  12.5 1.0 convolution_convert_fusion.1
  13.5 0.0 copy-start.8
  13.5 0.1 broadcast_in_dim.106
  13.6 0.8 pad_maximum_fusion.1
  14.4 6.4 %all-to-all-start = ((f16[16,72,128]{2,1,0:T(8,128)(2,1)}), f16[16,72,128]{2,1,0:T(8,128)(2,1)S(1)}, u32[]{:S(2)}, u32[]{:S(2)}) async-start(f16[16,72,128]{2,1,0:T(8,128)(2,1)} %pad_maximum_fusion.1), calls=%async_computation | async-start | bytes 589824 | tf_op jit(solution)/shard_map/all_to_all | solution.py:53
  20.9 0.3 convolution_convert_fusion.2
  21.2 5.6 %all-to-all-done = f16[16,72,128]{2,1,0:T(8,128)(2,1)S(1)} async-done(((f16[16,72,128]{2,1,0:T(8,128)(2,1)}), f16[16,72,128]{2,1,0:T(8,128)(2,1)S(1)}, u32[]{:S(2)}, u32[]{:S(2)}) %all-to-all-start) | async-done | bytes 294944 | tf_op jit(solution)/shard_map/all_to_all | solution.py:53
  26.9 0.1 add_convert_fusion.4
  26.9 11.0 %collective-permute-start = (f16[4,64,128]{2,1,0:T(8,128)(2,1)S(1)}, f16[4,64,128]{2,1,0:T(8,128)(2,1)S(1)}, u32[]{:S(2)}, u32[]{:S(2)}) collective-permute-start(f16[4,64,128]{2,1,0:T(8,128)(2,1)S(1)} %get-tuple-element.15), channel_id=1, source_target_pairs={{0,128},{32,160},{64,192},{96,224},{1,129},{33,161},{65,193},{97,2... | collective-permute-start | bytes 196616 | tf_op jit(solution)/shard_map/ppermute | solution.py:66
  37.9 2.1 %collective-permute-done = f16[4,64,128]{2,1,0:T(8,128)(2,1)S(1)} collective-permute-done((f16[4,64,128]{2,1,0:T(8,128)(2,1)S(1)}, f16[4,64,128]{2,1,0:T(8,128)(2,1)S(1)}, u32[]{:S(2)}, u32[]{:S(2)}) %collective-permute-start) | collective-permute-done | bytes 65568 | tf_op jit(solution)/shard_map/ppermute | solution.py:66
  40.1 0.7 collective-permute-start.1
  40.8 1.2 copy.93
  42.0 0.7 collective-permute-start.2
  42.7 0.1 fusion.51
  42.8 0.8 pad_maximum_fusion.2
  43.7 7.3 %all-to-all-start.1 = ((f16[16,64,128]{2,1,0:T(8,128)(2,1)}), f16[16,64,128]{2,1,0:T(8,128)(2,1)S(1)}, u32[]{:S(2)}, u32[]{:S(2)}) async-start(f16[16,64,128]{2,1,0:T(8,128)(2,1)} %pad_maximum_fusion.2), calls=%async_computation.1 | async-start | bytes 524288 | tf_op jit(solution)/shard_map/all_to_all | solution.py:72
  51.0 0.4 fusion.37
  51.4 0.0 copy-start.2
  51.4 6.1 %fusion.16 = f32[256,16,64]{0,2,1:T(8,128)} fusion(f32[256,16,64]{0,2,1:T(8,128)S(1)} %bitcast.177, f32[256,256]{1,0:T(8,128)S(1)} %fusion.37, f32[16,256]{1,0:T(8,128)S(1)} %get-tuple-element.28, pred[256,256]{1,0:T(8,128)(4,1)S(1)} %iota_compare_fusion.5, f32[16]{0:T(128)S(1)} %copy-done.8), kind=kOutput, calls=%fused_computation.16 | convolution fusion | flops 810024960 | bytes 2441280 | tf_op jit(solution)/shard_map/hij,jhp->ihp/dot_general | solution.py:214
  57.6 3.8 %all-to-all-done.1 = f16[16,64,128]{2,1,0:T(8,128)(2,1)S(1)} async-done(((f16[16,64,128]{2,1,0:T(8,128)(2,1)}), f16[16,64,128]{2,1,0:T(8,128)(2,1)S(1)}, u32[]{:S(2)}, u32[]{:S(2)}) %all-to-all-start.1) | async-done | bytes 262176 | tf_op jit(solution)/shard_map/all_to_all | solution.py:72
  61.3 3.2 %multiply_reduce_fusion.1 = (f32[256]{0:T(256)S(1)}, f32[256,16,64]{0,2,1:T(8,128)}) fusion(f32[256,16,64]{0,2,1:T(8,128)S(1)} %bitcast.181, f32[256,16,64]{0,2,1:T(8,128)} %fusion.16, f16[16,64,128]{2,1,0:T(8,128)(2,1)S(1)} %all-to-all-done.1, f32[1,256,128]{2,1,0:T(8,128)S(1)} %copy-done, f32[256,16]{0,1:T(8,128)S(1)} %get-tuple-element.25), kind=kOutput, calls=%fused_computation.31 | convolution fusion | flops 405012224 | bytes 3556352 | tf_op jit(solution)/shard_map/in,hpn->ihp/dot_general | solution.py:217
  64.6 1.6 copy.92
  66.2 1.8 multiply_reduce_fusion
  68.0 0.0 copy-start.6
  68.0 1.8 convolution_convert_fusion
  69.8 9.5 %all-to-all-start.2 = ((bf16[32,24,1024]{2,1,0:T(8,128)(2,1)}), bf16[32,24,1024]{2,1,0:T(8,128)(2,1)S(1)}, u32[]{:S(2)}, u32[]{:S(2)}) async-start(bf16[32,24,1024]{2,1,0:T(8,128)(2,1)} %bitcast.179), calls=%async_computation.2 | async-start | bytes 3145728 | tf_op jit(solution)/shard_map/all_to_all | solution.py:250
  79.4 0.3 add_convert_fusion.1
  79.7 0.1 pad_maximum_fusion.sel_ref
  79.8 22.2 %all-to-all-done.2 = bf16[32,24,1024]{2,1,0:T(8,128)(2,1)S(1)} async-done(((bf16[32,24,1024]{2,1,0:T(8,128)(2,1)}), bf16[32,24,1024]{2,1,0:T(8,128)(2,1)S(1)}, u32[]{:S(2)}, u32[]{:S(2)}) %all-to-all-start.2) | async-done | bytes 1572896 | tf_op jit(solution)/shard_map/all_to_all | solution.py:250
  102.0 32.7 %all-gather.3.cloned.1.call-done = bf16[9216,512]{1,0:T(8,128)(2,1)} async-done(((bf16[576,512]{1,0:T(8,128)(2,1)}), bf16[9216,512]{1,0:T(8,128)(2,1)}) %all-gather.3.cloned.1.call-update) | async-done | bytes 9437200 | tf_op jit(solution)/shard_map/all_gather | solution.py:197
  134.7 10.3 %shard_map.137 = bf16[768,1024]{1,0:T(8,128)(2,1)S(1)} custom-call(bf16[768,1024]{1,0:T(8,128)(2,1)S(1)} %bitcast.173, bf16[16,576,512]{2,1,0:T(8,128)(2,1)} %bitcast.176), custom_call_target="tpu_custom_call" | custom-call | tf_op jit(solution)/shard_map/pallas_call | solution.py:128
  145.1 31.9 %all_to_all.20 = bf16[32,24,1024]{2,1,0:T(8,128)(2,1)S(1)} all-to-all(bf16[32,24,1024]{2,1,0:T(8,128)(2,1)S(1)} %bitcast.175), channel_id=1, replica_groups=mesh['tm'=16,'expert'=32] {'expert'}, dimensions={0} | all-to-all | bytes 3145728 | tf_op jit(solution)/shard_map/all_to_all | solution.py:257
  177.0 1.8 shard_map.138
  (40 shorter events, 0.4 us)
Async XLA Ops:
  6.5 44.5 %copy-start = (f32[1,256,128]{2,1,0:T(8,128)S(1)}, f32[1,256,128]{2,1,0:T(8,128)}, u32[]{:S(2)}) copy-start(f32[1,256,128]{2,1,0:T(8,128)} %param.17) | copy-start | bytes 393220
  6.5 6.0 %copy-start.3 = (f32[1,256,128]{2,1,0:T(8,128)S(1)}, f32[1,256,128]{2,1,0:T(8,128)}, u32[]{:S(2)}) copy-start(f32[1,256,128]{2,1,0:T(8,128)} %param.16) | copy-start | bytes 393220
  6.5 128.2 %all-gather.3.cloned.1.call-start = ((), (), s32[]{:S(2)}) async-start(), calls=%async_computation.4 | async-start | bytes 10027008 | tf_op jit(solution)/shard_map/all_gather | solution.py:197
  6.5 14.3 %copy-start.4 = (s32[1,256,2]{1,2,0:T(2,128)S(1)}, s32[1,256,2]{1,2,0:T(2,128)}, u32[]{:S(2)}) copy-start(s32[1,256,2]{1,2,0:T(2,128)} %param.26) | copy-start | bytes 6148
  10.7 30.0 %copy-start.1 = (bf16[1,256,1024]{2,1,0:T(8,128)(2,1)S(1)}, bf16[1,256,1024]{2,1,0:T(8,128)(2,1)}, u32[]{:S(2)}) copy-start(bf16[1,256,1024]{2,1,0:T(8,128)(2,1)} %param.15) | copy-start | bytes 1572868
  13.5 37.9 %copy-start.8 = (f32[16]{0:T(128)S(1)}, f32[16]{0:T(128)}, u32[]{:S(2)}) copy-start(f32[16]{0:T(128)} %param.19) | copy-start | bytes 196
  14.4 12.3 %all-to-all-start = ((f16[16,72,128]{2,1,0:T(8,128)(2,1)}), f16[16,72,128]{2,1,0:T(8,128)(2,1)S(1)}, u32[]{:S(2)}, u32[]{:S(2)}) async-start(f16[16,72,128]{2,1,0:T(8,128)(2,1)} %pad_maximum_fusion.1), calls=%async_computation | async-start | bytes 589824 | tf_op jit(solution)/shard_map/all_to_all | solution.py:53
  26.9 13.1 %collective-permute-start = (f16[4,64,128]{2,1,0:T(8,128)(2,1)S(1)}, f16[4,64,128]{2,1,0:T(8,128)(2,1)S(1)}, u32[]{:S(2)}, u32[]{:S(2)}) collective-permute-start(f16[4,64,128]{2,1,0:T(8,128)(2,1)S(1)} %get-tuple-element.15), channel_id=1, source_target_pairs={{0,128},{32,160},{64,192},{96,224},{1,129},{33,161},{65,193},{97,2... | collective-permute-start | bytes 196616 | tf_op jit(solution)/shard_map/ppermute | solution.py:66
  40.1 1.9 %collective-permute-start.1 = (f16[4,64,128]{2,1,0:T(8,128)(2,1)S(1)}, f16[4,64,128]{2,1,0:T(8,128)(2,1)S(1)}, u32[]{:S(2)}, u32[]{:S(2)}) collective-permute-start(f16[4,64,128]{2,1,0:T(8,128)(2,1)S(1)} %fusion.33), channel_id=1, source_target_pairs={{128,256},{160,288},{192,320},{224,352},{129,257},{161,289},{193,3... | collective-permute-start | bytes 196616 | tf_op jit(solution)/shard_map/ppermute | solution.py:66
  42.0 0.7 collective-permute-start.2
  43.7 17.7 %all-to-all-start.1 = ((f16[16,64,128]{2,1,0:T(8,128)(2,1)}), f16[16,64,128]{2,1,0:T(8,128)(2,1)S(1)}, u32[]{:S(2)}, u32[]{:S(2)}) async-start(f16[16,64,128]{2,1,0:T(8,128)(2,1)} %pad_maximum_fusion.2), calls=%async_computation.1 | async-start | bytes 524288 | tf_op jit(solution)/shard_map/all_to_all | solution.py:72
  51.4 9.9 %copy-start.2 = (f32[1,256,1024]{1,2,0:T(8,128)S(1)}, f32[1,256,1024]{1,2,0:T(8,128)}, u32[]{:S(2)}) copy-start(f32[1,256,1024]{1,2,0:T(8,128)} %copy.93) | copy-start | bytes 3145732
  57.6 8.6 %copy-start.5 = (f32[1024]{0:T(1024)S(1)}, f32[1024]{0:T(1024)}, u32[]{:S(2)}) copy-start(f32[1024]{0:T(1024)} %param.21) | copy-start | bytes 12292
  64.6 3.4 %copy-start.7 = (f32[1024]{0:T(1024)S(1)}, f32[1024]{0:T(1024)}, u32[]{:S(2)}) copy-start(f32[1024]{0:T(1024)} %param.22) | copy-start | bytes 12292
  68.0 11.4 %copy-start.6 = (f32[1,256,2]{1,2,0:T(2,128)S(1)}, f32[1,256,2]{1,2,0:T(2,128)}, u32[]{:S(2)}) copy-start(f32[1,256,2]{1,2,0:T(2,128)} %param.27) | copy-start | bytes 6148
  69.8 32.2 %all-to-all-start.2 = ((bf16[32,24,1024]{2,1,0:T(8,128)(2,1)}), bf16[32,24,1024]{2,1,0:T(8,128)(2,1)S(1)}, u32[]{:S(2)}, u32[]{:S(2)}) async-start(bf16[32,24,1024]{2,1,0:T(8,128)(2,1)} %bitcast.179), calls=%async_computation.2 | async-start | bytes 3145728 | tf_op jit(solution)/shard_map/all_to_all | solution.py:250
Sparse Core Ops, SparseCore 0:
  9.4 125.2 all-gather.2

commit v7 on v5

--- a/solution.py
+++ b/solution.py
@@ -237,6 +237,7 @@
     received = lax.all_to_all(
         outgoing.reshape(experts, capacity, model_width), "expert", 0, 0, tiled=True
     )
+    received, selection = lax.optimization_barrier((received, selection))
     produced = expert_layer(
         received.reshape(experts * capacity, model_width), gathered, model_width, hidden_width
     )

time: 187 us -> 186 us (level)
  transfers between devices with their start and end apart: 7 -> 7, of which waited for: 5 -> 5; matrix products, arithmetic and copies ran while one was open for 12% -> 13% of each run, Pallas kernels for 0% -> 0%
where the time goes in v7:
time: 186 us; the launch traced here: 185 us
  waiting for transfers between devices  66.4 us (36%)
  starting transfers between devices  35.6 us (19%)
  blocking collectives  31.9 us (17%)
  Pallas kernels  13.7 us (7%)
  between operations  13.7 us (7%)
  matrix products  12.8 us (7%)
  local copies, waits for them, and re-layouts  5.95 us (3%)
  other arithmetic  5.02 us (3%)
    all_gather x1, waiting for transfers between devices, per_device(): lax.all_gather(pack_weights(w_gate[0], w_up[0], w_down[0]), 'tm', axis=0)  32.7 us
    all_to_all x1, blocking collectives, per_device(): lax.all_to_all(produced.reshape(experts, capacity, model_width), 'expert'...  31.9 us
    all_to_all x1, waiting for transfers between devices, per_device(): lax.all_to_all(outgoing.reshape(experts, capacity, model_width), 'expert'...  22.2 us
    ppermute x3, starting transfers between devices, incoming_states(): handed = lax.ppermute((passed * entry + total).astype(f16), 'tm', hops)  12.3 us
    pallas_call x1, Pallas kernels, expert_layer(): pl.pallas_call(body, in_specs=[in_vmem, pl.BlockSpec(memory_space=pl.ANY)...  9.81 us
    all_to_all x1, starting transfers between devices, per_device(): lax.all_to_all(outgoing.reshape(experts, capacity, model_width), 'expert'...  9.54 us
    all_to_all x1, starting transfers between devices, incoming_states(): lax.all_to_all(returned, 'tm', 0, 0, tiled=True, axis_index_groups=groups)  7.35 us
    all_to_all x1, starting transfers between devices, incoming_states(): lax.all_to_all(sent, 'tm', 0, 0, tiled=True, axis_index_groups=groups)  6.44 us
  transfers between devices with their start and end apart: 7, of which 5 were waited for; matrix products, arithmetic and copies ran while one was open for 13% of the time, Pallas kernels for 0%

profile of v7, /device:TPU:1, one launch (start us, length us, event | category | flops | bytes accessed | tf_op | source)
XLA Modules:
  0.0 185.2 jit_solution(2940682875099003286)
XLA Ops:
  6.5 2.0 %shard_map.136 = bf16[576,512]{1,0:T(8,128)(2,1)} custom-call(bf16[64,1536]{1,0:T(8,128)(2,1)} %bitcast.183, bf16[64,1536]{1,0:T(8,128)(2,1)} %bitcast.184, bf16[96,1024]{1,0:T(8,128)(2,1)} %bitcast.185), custom_call_target="tpu_custom_call" | custom-call | tf_op jit(solution)/shard_map/pallas_call | solution.py:35
  8.6 0.0 all-gather.3.cloned.1.call-update
  8.6 0.7 copy_bitcast_fusion.1
  9.3 0.6 reduce-window.6
  9.9 0.2 slice_reduce_fusion
  10.1 0.1 fusion.49
  10.2 0.2 slice_reduce_fusion.1
  10.4 0.1 copy.86
  10.5 0.1 copy.87
  10.6 0.1 copy.88
  10.6 0.1 stack.16
  10.7 0.0 copy-start.1
  10.7 1.6 copy.84
  12.4 0.1 bitcast_exponential_fusion
  12.4 0.1 bitcast_multiply_fusion.1
  12.5 1.0 convolution_convert_fusion.1
  13.5 0.0 copy-start.8
  13.5 0.1 broadcast_in_dim.106
  13.6 0.8 pad_maximum_fusion.1
  14.4 6.4 %all-to-all-start = ((f16[16,72,128]{2,1,0:T(8,128)(2,1)}), f16[16,72,128]{2,1,0:T(8,128)(2,1)S(1)}, u32[]{:S(2)}, u32[]{:S(2)}) async-start(f16[16,72,128]{2,1,0:T(8,128)(2,1)} %pad_maximum_fusion.1), calls=%async_computation | async-start | bytes 589824 | tf_op jit(solution)/shard_map/all_to_all | solution.py:53
  20.9 0.3 convolution_convert_fusion.2
  21.2 5.6 %all-to-all-done = f16[16,72,128]{2,1,0:T(8,128)(2,1)S(1)} async-done(((f16[16,72,128]{2,1,0:T(8,128)(2,1)}), f16[16,72,128]{2,1,0:T(8,128)(2,1)S(1)}, u32[]{:S(2)}, u32[]{:S(2)}) %all-to-all-start) | async-done | bytes 294944 | tf_op jit(solution)/shard_map/all_to_all | solution.py:53
  26.9 0.1 add_convert_fusion.4
  26.9 11.0 %collective-permute-start = (f16[4,64,128]{2,1,0:T(8,128)(2,1)S(1)}, f16[4,64,128]{2,1,0:T(8,128)(2,1)S(1)}, u32[]{:S(2)}, u32[]{:S(2)}) collective-permute-start(f16[4,64,128]{2,1,0:T(8,128)(2,1)S(1)} %get-tuple-element.15), channel_id=1, source_target_pairs={{0,128},{32,160},{64,192},{96,224},{1,129},{33,161},{65,193},{97,2... | collective-permute-start | bytes 196616 | tf_op jit(solution)/shard_map/ppermute | solution.py:66
  37.9 2.1 %collective-permute-done = f16[4,64,128]{2,1,0:T(8,128)(2,1)S(1)} collective-permute-done((f16[4,64,128]{2,1,0:T(8,128)(2,1)S(1)}, f16[4,64,128]{2,1,0:T(8,128)(2,1)S(1)}, u32[]{:S(2)}, u32[]{:S(2)}) %collective-permute-start) | collective-permute-done | bytes 65568 | tf_op jit(solution)/shard_map/ppermute | solution.py:66
  40.1 0.7 collective-permute-start.1
  40.8 1.2 copy.93
  42.0 0.7 collective-permute-start.2
  42.7 0.1 fusion.51
  42.8 0.8 pad_maximum_fusion.2
  43.7 7.3 %all-to-all-start.1 = ((f16[16,64,128]{2,1,0:T(8,128)(2,1)}), f16[16,64,128]{2,1,0:T(8,128)(2,1)S(1)}, u32[]{:S(2)}, u32[]{:S(2)}) async-start(f16[16,64,128]{2,1,0:T(8,128)(2,1)} %pad_maximum_fusion.2), calls=%async_computation.1 | async-start | bytes 524288 | tf_op jit(solution)/shard_map/all_to_all | solution.py:72
  51.0 0.4 fusion.37
  51.4 0.0 copy-start.2
  51.4 6.1 %fusion.16 = f32[256,16,64]{0,2,1:T(8,128)} fusion(f32[256,16,64]{0,2,1:T(8,128)S(1)} %bitcast.177, f32[256,256]{1,0:T(8,128)S(1)} %fusion.37, f32[16,256]{1,0:T(8,128)S(1)} %get-tuple-element.28, pred[256,256]{1,0:T(8,128)(4,1)S(1)} %iota_compare_fusion.5, f32[16]{0:T(128)S(1)} %copy-done.8), kind=kOutput, calls=%fused_computation.16 | convolution fusion | flops 810024960 | bytes 2441280 | tf_op jit(solution)/shard_map/hij,jhp->ihp/dot_general | solution.py:201
  57.6 3.8 %all-to-all-done.1 = f16[16,64,128]{2,1,0:T(8,128)(2,1)S(1)} async-done(((f16[16,64,128]{2,1,0:T(8,128)(2,1)}), f16[16,64,128]{2,1,0:T(8,128)(2,1)S(1)}, u32[]{:S(2)}, u32[]{:S(2)}) %all-to-all-start.1) | async-done | bytes 262176 | tf_op jit(solution)/shard_map/all_to_all | solution.py:72
  61.3 3.2 %multiply_reduce_fusion.1 = (f32[256]{0:T(256)S(1)}, f32[256,16,64]{0,2,1:T(8,128)}) fusion(f32[256,16,64]{0,2,1:T(8,128)S(1)} %bitcast.181, f32[256,16,64]{0,2,1:T(8,128)} %fusion.16, f16[16,64,128]{2,1,0:T(8,128)(2,1)S(1)} %all-to-all-done.1, f32[1,256,128]{2,1,0:T(8,128)S(1)} %copy-done, f32[256,16]{0,1:T(8,128)S(1)} %get-tuple-element.25), kind=kOutput, calls=%fused_computation.31 | convolution fusion | flops 405012224 | bytes 3556352 | tf_op jit(solution)/shard_map/in,hpn->ihp/dot_general | solution.py:204
  64.6 1.6 copy.92
  66.2 1.8 multiply_reduce_fusion
  68.0 0.0 copy-start.6
  68.0 1.8 convolution_convert_fusion
  69.8 9.5 %all-to-all-start.2 = ((bf16[32,24,1024]{2,1,0:T(8,128)(2,1)}), bf16[32,24,1024]{2,1,0:T(8,128)(2,1)S(1)}, u32[]{:S(2)}, u32[]{:S(2)}) async-start(bf16[32,24,1024]{2,1,0:T(8,128)(2,1)} %bitcast.179), calls=%async_computation.2 | async-start | bytes 3145728 | tf_op jit(solution)/shard_map/all_to_all | solution.py:237
  79.4 0.3 add_convert_fusion.1
  79.7 0.1 pad_maximum_fusion.sel_ref
  79.8 22.2 %all-to-all-done.2 = bf16[32,24,1024]{2,1,0:T(8,128)(2,1)S(1)} async-done(((bf16[32,24,1024]{2,1,0:T(8,128)(2,1)}), bf16[32,24,1024]{2,1,0:T(8,128)(2,1)S(1)}, u32[]{:S(2)}, u32[]{:S(2)}) %all-to-all-start.2) | async-done | bytes 1572896 | tf_op jit(solution)/shard_map/all_to_all | solution.py:237
  102.0 32.7 %all-gather.3.cloned.1.call-done = bf16[9216,512]{1,0:T(8,128)(2,1)} async-done(((bf16[576,512]{1,0:T(8,128)(2,1)}), bf16[9216,512]{1,0:T(8,128)(2,1)}) %all-gather.3.cloned.1.call-update) | async-done | bytes 9437200 | tf_op jit(solution)/shard_map/all_gather | solution.py:184
  134.7 9.8 %shard_map.137 = bf16[768,1024]{1,0:T(8,128)(2,1)S(1)} custom-call(bf16[768,1024]{1,0:T(8,128)(2,1)S(1)} %bitcast.173, bf16[16,576,512]{2,1,0:T(8,128)(2,1)} %bitcast.176), custom_call_target="tpu_custom_call" | custom-call | tf_op jit(solution)/shard_map/pallas_call | solution.py:117
  144.6 31.9 %all_to_all.20 = bf16[32,24,1024]{2,1,0:T(8,128)(2,1)S(1)} all-to-all(bf16[32,24,1024]{2,1,0:T(8,128)(2,1)S(1)} %bitcast.175), channel_id=1, replica_groups=mesh['tm'=16,'expert'=32] {'expert'}, dimensions={0} | all-to-all | bytes 3145728 | tf_op jit(solution)/shard_map/all_to_all | solution.py:244
  176.5 1.8 shard_map.138
  (40 shorter events, 0.4 us)
Async XLA Ops:
  6.5 44.5 %copy-start = (f32[1,256,128]{2,1,0:T(8,128)S(1)}, f32[1,256,128]{2,1,0:T(8,128)}, u32[]{:S(2)}) copy-start(f32[1,256,128]{2,1,0:T(8,128)} %param.17) | copy-start | bytes 393220
  6.5 6.0 %copy-start.3 = (f32[1,256,128]{2,1,0:T(8,128)S(1)}, f32[1,256,128]{2,1,0:T(8,128)}, u32[]{:S(2)}) copy-start(f32[1,256,128]{2,1,0:T(8,128)} %param.16) | copy-start | bytes 393220
  6.5 128.2 %all-gather.3.cloned.1.call-start = ((), (), s32[]{:S(2)}) async-start(), calls=%async_computation.4 | async-start | bytes 10027008 | tf_op jit(solution)/shard_map/all_gather | solution.py:184
  6.5 14.3 %copy-start.4 = (s32[1,256,2]{1,2,0:T(2,128)S(1)}, s32[1,256,2]{1,2,0:T(2,128)}, u32[]{:S(2)}) copy-start(s32[1,256,2]{1,2,0:T(2,128)} %param.26) | copy-start | bytes 6148
  10.7 30.0 %copy-start.1 = (bf16[1,256,1024]{2,1,0:T(8,128)(2,1)S(1)}, bf16[1,256,1024]{2,1,0:T(8,128)(2,1)}, u32[]{:S(2)}) copy-start(bf16[1,256,1024]{2,1,0:T(8,128)(2,1)} %param.15) | copy-start | bytes 1572868
  13.5 37.9 %copy-start.8 = (f32[16]{0:T(128)S(1)}, f32[16]{0:T(128)}, u32[]{:S(2)}) copy-start(f32[16]{0:T(128)} %param.19) | copy-start | bytes 196
  14.4 12.3 %all-to-all-start = ((f16[16,72,128]{2,1,0:T(8,128)(2,1)}), f16[16,72,128]{2,1,0:T(8,128)(2,1)S(1)}, u32[]{:S(2)}, u32[]{:S(2)}) async-start(f16[16,72,128]{2,1,0:T(8,128)(2,1)} %pad_maximum_fusion.1), calls=%async_computation | async-start | bytes 589824 | tf_op jit(solution)/shard_map/all_to_all | solution.py:53
  26.9 13.1 %collective-permute-start = (f16[4,64,128]{2,1,0:T(8,128)(2,1)S(1)}, f16[4,64,128]{2,1,0:T(8,128)(2,1)S(1)}, u32[]{:S(2)}, u32[]{:S(2)}) collective-permute-start(f16[4,64,128]{2,1,0:T(8,128)(2,1)S(1)} %get-tuple-element.15), channel_id=1, source_target_pairs={{0,128},{32,160},{64,192},{96,224},{1,129},{33,161},{65,193},{97,2... | collective-permute-start | bytes 196616 | tf_op jit(solution)/shard_map/ppermute | solution.py:66
  40.1 1.9 %collective-permute-start.1 = (f16[4,64,128]{2,1,0:T(8,128)(2,1)S(1)}, f16[4,64,128]{2,1,0:T(8,128)(2,1)S(1)}, u32[]{:S(2)}, u32[]{:S(2)}) collective-permute-start(f16[4,64,128]{2,1,0:T(8,128)(2,1)S(1)} %fusion.33), channel_id=1, source_target_pairs={{128,256},{160,288},{192,320},{224,352},{129,257},{161,289},{193,3... | collective-permute-start | bytes 196616 | tf_op jit(solution)/shard_map/ppermute | solution.py:66
  42.0 0.7 collective-permute-start.2
  43.7 17.7 %all-to-all-start.1 = ((f16[16,64,128]{2,1,0:T(8,128)(2,1)}), f16[16,64,128]{2,1,0:T(8,128)(2,1)S(1)}, u32[]{:S(2)}, u32[]{:S(2)}) async-start(f16[16,64,128]{2,1,0:T(8,128)(2,1)} %pad_maximum_fusion.2), calls=%async_computation.1 | async-start | bytes 524288 | tf_op jit(solution)/shard_map/all_to_all | solution.py:72
  51.4 9.9 %copy-start.2 = (f32[1,256,1024]{1,2,0:T(8,128)S(1)}, f32[1,256,1024]{1,2,0:T(8,128)}, u32[]{:S(2)}) copy-start(f32[1,256,1024]{1,2,0:T(8,128)} %copy.93) | copy-start | bytes 3145732
  57.6 8.6 %copy-start.5 = (f32[1024]{0:T(1024)S(1)}, f32[1024]{0:T(1024)}, u32[]{:S(2)}) copy-start(f32[1024]{0:T(1024)} %param.21) | copy-start | bytes 12292
  64.6 3.4 %copy-start.7 = (f32[1024]{0:T(1024)S(1)}, f32[1024]{0:T(1024)}, u32[]{:S(2)}) copy-start(f32[1024]{0:T(1024)} %param.22) | copy-start | bytes 12292
  68.0 11.4 %copy-start.6 = (f32[1,256,2]{1,2,0:T(2,128)S(1)}, f32[1,256,2]{1,2,0:T(2,128)}, u32[]{:S(2)}) copy-start(f32[1,256,2]{1,2,0:T(2,128)} %param.27) | copy-start | bytes 6148
  69.8 32.2 %all-to-all-start.2 = ((bf16[32,24,1024]{2,1,0:T(8,128)(2,1)}), bf16[32,24,1024]{2,1,0:T(8,128)(2,1)S(1)}, u32[]{:S(2)}, u32[]{:S(2)}) async-start(bf16[32,24,1024]{2,1,0:T(8,128)(2,1)} %bitcast.179), calls=%async_computation.2 | async-start | bytes 3145728 | tf_op jit(solution)/shard_map/all_to_all | solution.py:237
Sparse Core Ops, SparseCore 0:
  9.4 125.2 all-gather.2
